TPU v7x, 512 devices: a whole 4x8x8 slice. The times are simulated.
512 devices in a mesh: space: 256 (over z, y, x), wt: 2 (over core).
Axes of the slice: x: 4, y: 8, z: 8, core: 2. Of those that a mesh axis runs over, the one named last changes fastest.
Arguments:
- features: bfloat16 [512, 8, 8, 8, 192], P(('space', 'wt')), may hold values from -6 to 6
- occupancy: int32 [512], P(('space', 'wt')), may hold values from 0 to 1, as said below
- neighbours: int32 [512, 27], P(('space', 'wt')), may hold values from -1 to 511, as said below
- kernel_one: bfloat16 [3, 3, 3, 48, 768], P(None, None, None, None, 'wt'), may hold values from -0.078125 to 0.078125
- kernel_two: bfloat16 [3, 3, 3, 48, 768], P(None, None, None, None, 'wt'), may hold values from -0.078125 to 0.078125
Outputs:
- block_out: float32 [512, 8, 8, 8, 192], P(('space', 'wt'))
Inputs may be any that keep to these rules, and one draw needn't show every extreme that they name: `occupancy`: the first slot of every device's 1 slots is active; the others are active with probability three quarters. `neighbours`: entries are -1 or an active slot; for an active slot s, entry 13 is s itself, and every other entry lies among the slots of the same device, the previous or the next device in slot order (slots d * 1 to (d+1) - 1 belong to device d). Rows of inactive slots are all -1.
All inputs are finite; a program needn't handle non-finite values.
Results may differ from a plain program's by a relative error of at most 0.0018.
Values may be sent and summed in bfloat16 or wider, within the bound.
A program may use at most 64 MiB of HBM per device.

v0:
```python
import jax
import jax.numpy as jnp
from jax import lax
from jax.sharding import PartitionSpec as P

C = 192


def extended(value, sides, width):
    for axis, dim in sides:
        size, length = (lax.axis_size(axis), value.shape[dim])
        up = [(i, (i + 1) % size) for i in range(size - 1)]
        down = [(j, i) for i, j in up]
        last = lax.slice_in_dim(value, length - width, length, axis=dim)
        leading = lax.slice_in_dim(value, 0, width, axis=dim)
        before = lax.ppermute(last, axis, up)
        after = lax.ppermute(leading, axis, down)
        value = jnp.concatenate([before, value, after], axis=dim)
    return value


def unpack_kernel(stored):
    quarter = stored.shape[3]
    width = C
    groups = stored.shape[4] // width
    grouped = stored.reshape(3, 3, 3, quarter, groups, width)
    return jnp.transpose(grouped, (0, 1, 2, 4, 3, 5)).reshape(3, 3, 3, groups * quarter, width)


def pad_blocks(source, index):
    ranges = ((7, 8), (0, 8), (0, 1))
    planes = []
    for first in range(3):
        rows = []
        for second in range(3):
            cols = []
            for third in range(3):
                tap = first * 9 + second * 3 + third
                which = index[:, tap]
                picked = jnp.take(source, jnp.maximum(which, 0), axis=0)
                lo_a, hi_a = ranges[first]
                lo_b, hi_b = ranges[second]
                lo_c, hi_c = ranges[third]
                piece = picked[:, lo_a:hi_a, lo_b:hi_b, lo_c:hi_c, :]
                valid = (which >= 0)[:, None, None, None, None]
                cols.append(jnp.where(valid, piece, jnp.zeros((), piece.dtype)))
            rows.append(jnp.concatenate(cols, axis=3))
        planes.append(jnp.concatenate(rows, axis=2))
    return jnp.concatenate(planes, axis=1)


def conv_taps(padded, kernel):
    return lax.conv_general_dilated(
        padded,
        kernel,
        (1, 1, 1),
        "VALID",
        dimension_numbers=("NDHWC", "DHWIO", "NDHWC"),
        preferred_element_type=jnp.float32,
    )


def padded_field(source, local_index):
    count = source.shape[0]
    beside_all = extended(source, ((("space", "wt"), 0),), count)
    return pad_blocks(beside_all, local_index)


def convolve(padded, kernel):
    gathered = lax.all_gather(kernel, "wt", axis=4, tiled=True)
    return conv_taps(padded, unpack_kernel(gathered))


def body(features, occupancy, neighbours, kernel_one, kernel_two):
    count = features.shape[0]
    device = lax.axis_index(("space", "wt"))
    local_index = jnp.where(neighbours >= 0, neighbours - (device - 1) * count, -1)
    active = occupancy.astype(jnp.float32)[:, None, None, None, None]
    hidden = (
        jax.nn.relu(convolve(padded_field(features, local_index), kernel_one)) * active
    ).astype(jnp.bfloat16)
    second = convolve(padded_field(hidden, local_index), kernel_two)
    return jax.nn.relu(features.astype(jnp.float32) + second) * active


def solution(mesh):
    return jax.shard_map(
        body,
        mesh=mesh,
        in_specs=(
            P(("space", "wt"), None, None, None, None),
            P(("space", "wt")),
            P(("space", "wt"), None),
            P(None, None, None, None, "wt"),
            P(None, None, None, None, "wt"),
        ),
        out_specs=P(("space", "wt"), None, None, None, None),
        check_vma=False,
    )
```

profile of v0, /device:TPU:255, one launch (start us, length us, event | category | flops | bytes accessed | tf_op | source)
XLA Modules:
  0.0 107.6 jit_solution(8445054417161292691)
XLA Ops:
  6.5 0.7 all-gather.3.cloned.1.call-update
  7.3 4.9 %collective-permute-start = (bf16[1,8,8,8,192]{4,3,2,1,0:T(8,128)(2,1)}, bf16[1,8,8,8,192]{4,3,2,1,0:T(8,128)(2,1)S(1)}, u32[]{:S(2)}, u32[]{:S(2)}) collective-permute-start(bf16[1,8,8,8,192]{4,3,2,1,0:T(8,128)(2,1)} %param.7), channel_id=1, source_target_pairs={{0,1},{1,2},{2,3},{3,4},{4,5},{5,6},{6,7},{7,8},{8,9},{9,10},{10,1... | collective-permute-start | bytes 589832 | tf_op jit(solution)/shard_map/ppermute | solution.py:16
  12.2 1.9 %collective-permute-start.1 = (bf16[1,8,8,8,192]{4,3,2,1,0:T(8,128)(2,1)}, bf16[1,8,8,8,192]{4,3,2,1,0:T(8,128)(2,1)S(1)}, u32[]{:S(2)}, u32[]{:S(2)}) collective-permute-start(bf16[1,8,8,8,192]{4,3,2,1,0:T(8,128)(2,1)} %param.7), channel_id=1, source_target_pairs={{1,0},{2,1},{3,2},{4,3},{5,4},{6,5},{7,6},{8,7},{9,8},{10,9},{11,1... | collective-permute-start | bytes 589832 | tf_op jit(solution)/shard_map/ppermute | solution.py:17
  14.2 0.7 fusion.32
  27.5 0.7 fusion.33
  50.5 0.1 broadcast_select_fusion.35
  50.5 0.1 broadcast_select_fusion.39
  50.7 0.2 broadcast_select_fusion.7
  51.0 1.5 %maximum_maximum_fusion = bf16[1,10,10,10,192]{4,3,2,1,0:T(8,128)(2,1)} fusion(bf16[1,1,1,1,192]{4,3,2,1,0:T(2,128)(2,1)S(1)} %get-tuple-element.44, bf16[1,1,1,8,192]{4,3,2,1,0:T(8,128)(2,1)S(1)} %get-tuple-element.49, bf16[1,1,1,1,192]{4,3,2,1,0:T(2,128)(2,1)S(1)} %get-tuple-element.45, bf16[1,1,8,1,192]{4,3,2,1,0:T(2,128)(2,1)S(1)} %get-tuple-element.56, ...), kind=kLoop, calls=%fused_computation.4 | loop fusion | flops 10368000 | bytes 768000 | tf_op jit(solution)/shard_map/concatenate | solution.py:49
  52.5 5.2 %reshape.242 = bf16[3,3,3,48,4,192]{5,4,3,2,1,0:T(4,128)(2,1)S(1)} reshape(bf16[3,3,3,48,768]{4,3,2,1,0:T(8,128)(2,1)} %all-gather.3.cloned.1.call-done) | data formatting | bytes 3981312 | tf_op jit(solution)/shard_map/reshape | solution.py:26
  57.8 0.5 copy.13
  58.2 0.7 copy-done.1
  58.9 8.0 %fusion.2 = f32[1,8,8,8,192]{4,0,3,2,1:T(1,128)S(1)} fusion(bf16[3,3,3,192,192]{4,3,2,1,0:T(8,128)(2,1)S(1)} %bitcast.122, bf16[1,10,10,10,192]{4,3,2,1,0:T(8,128)(2,1)S(1)} %copy-done.1), kind=kOutput, calls=%fused_computation.2 | convolution fusion | flops 1019215872 | bytes 2767872 | tf_op jit(solution)/shard_map/conv_general_dilated | solution.py:53
  66.9 9.1 %collective-permute-start.2 = (bf16[1,8,8,8,192]{4,3,2,1,0:T(8,128)(2,1)S(1)}, bf16[1,8,8,8,192]{4,3,2,1,0:T(8,128)(2,1)S(1)}, u32[]{:S(2)}, u32[]{:S(2)}) collective-permute-start(bf16[1,8,8,8,192]{4,3,2,1,0:T(8,128)(2,1)S(1)} %fusion.7), channel_id=1, source_target_pairs={{0,1},{1,2},{2,3},{3,4},{4,5},{5,6},{6,7},{7,8},{8,9},{9,10},{10,1... | collective-permute-start | bytes 589832 | tf_op jit(solution)/shard_map/ppermute | solution.py:16
  76.0 2.1 %collective-permute-start.3 = (bf16[1,8,8,8,192]{4,3,2,1,0:T(8,128)(2,1)S(1)}, bf16[1,8,8,8,192]{4,3,2,1,0:T(8,128)(2,1)}, u32[]{:S(2)}, u32[]{:S(2)}) collective-permute-start(bf16[1,8,8,8,192]{4,3,2,1,0:T(8,128)(2,1)S(1)} %fusion.7), channel_id=1, source_target_pairs={{1,0},{2,1},{3,2},{4,3},{5,4},{6,5},{7,6},{8,7},{9,8},{10,9},{11,1... | collective-permute-start | bytes 589832 | tf_op jit(solution)/shard_map/ppermute | solution.py:17
  78.2 5.2 %reshape.244 = bf16[3,3,3,48,4,192]{5,4,3,2,1,0:T(4,128)(2,1)S(1)} reshape(bf16[3,3,3,48,768]{4,3,2,1,0:T(8,128)(2,1)} %all-gather.5.cloned.1.call-done) | data formatting | bytes 3981312 | tf_op jit(solution)/shard_map/reshape | solution.py:26
  83.4 0.5 copy.16
  83.9 5.5 %collective-permute-done.3 = bf16[1,8,8,8,192]{4,3,2,1,0:T(8,128)(2,1)} collective-permute-done((bf16[1,8,8,8,192]{4,3,2,1,0:T(8,128)(2,1)S(1)}, bf16[1,8,8,8,192]{4,3,2,1,0:T(8,128)(2,1)}, u32[]{:S(2)}, u32[]{:S(2)}) %collective-permute-start.3) | collective-permute-done | bytes 196640 | tf_op jit(solution)/shard_map/ppermute | solution.py:17
  89.4 1.1 %pad_maximum_fusion = bf16[3,8,8,8,192]{4,3,2,1,0:T(8,128)(2,1)S(1)} fusion(bf16[1,8,8,8,192]{4,3,2,1,0:T(8,128)(2,1)} %collective-permute-done.3, bf16[1,8,8,8,192]{4,3,2,1,0:T(8,128)(2,1)S(1)} %fusion.7, bf16[1,8,8,8,192]{4,3,2,1,0:T(8,128)(2,1)S(1)} %collective-permute-done.2), kind=kLoop, calls=%fused_computation.6 | loop fusion | flops 589824 | bytes 1179648 | tf_op jit(solution)/shard_map/concatenate | solution.py:18
  90.6 0.2 broadcast_select_fusion.6
  90.9 0.1 broadcast_select_fusion.34
  91.1 0.7 maximum_maximum_fusion.1
  91.8 8.1 %fusion = f32[1,8,8,8,192]{4,0,3,2,1:T(1,128)S(1)} fusion(bf16[3,3,3,192,192]{4,3,2,1,0:T(8,128)(2,1)S(1)} %bitcast.121, bf16[1,10,10,10,192]{4,3,2,1,0:T(8,128)(2,1)S(1)} %maximum_maximum_fusion.1), kind=kOutput, calls=%fused_computation | convolution fusion | flops 1019215872 | bytes 2767872 | tf_op jit(solution)/shard_map/conv_general_dilated | solution.py:53
  99.9 0.9 fusion.5
  (31 shorter events, 0.6 us)
Async XLA Ops:
  6.5 43.8 %copy-start = (bf16[1,8,8,8,192]{4,3,2,1,0:T(8,128)(2,1)S(1)}, bf16[1,8,8,8,192]{4,3,2,1,0:T(8,128)(2,1)}, u32[]{:S(2)}) copy-start(bf16[1,8,8,8,192]{4,3,2,1,0:T(8,128)(2,1)} %param.7) | copy-start | bytes 589828
  6.5 7.6 %copy-start.2 = (s32[1,27]{1,0:T(1,128)S(1)}, s32[1,27]{1,0:T(1,128)}, u32[]{:S(2)}) copy-start(s32[1,27]{1,0:T(1,128)} %param.9) | copy-start | bytes 328
  6.5 46.0 %all-gather.3.cloned.1.call-start = ((), (), s32[]{:S(2)}) async-start(), calls=%async_computation | async-start | bytes 2985984 | tf_op jit(solution)/shard_map/all_gather | solution.py:70
  7.3 70.9 %all-gather.5.cloned.1.call-start = ((), (), s32[]{:S(2)}) async-start(), calls=%async_computation.1 | async-start | bytes 2985984 | tf_op jit(solution)/shard_map/all_gather | solution.py:70
  7.3 43.0 %collective-permute-start = (bf16[1,8,8,8,192]{4,3,2,1,0:T(8,128)(2,1)}, bf16[1,8,8,8,192]{4,3,2,1,0:T(8,128)(2,1)S(1)}, u32[]{:S(2)}, u32[]{:S(2)}) collective-permute-start(bf16[1,8,8,8,192]{4,3,2,1,0:T(8,128)(2,1)} %param.7), channel_id=1, source_target_pairs={{0,1},{1,2},{2,3},{3,4},{4,5},{5,6},{6,7},{7,8},{8,9},{9,10},{10,1... | collective-permute-start | bytes 589832 | tf_op jit(solution)/shard_map/ppermute | solution.py:16
  12.2 38.2 %collective-permute-start.1 = (bf16[1,8,8,8,192]{4,3,2,1,0:T(8,128)(2,1)}, bf16[1,8,8,8,192]{4,3,2,1,0:T(8,128)(2,1)S(1)}, u32[]{:S(2)}, u32[]{:S(2)}) collective-permute-start(bf16[1,8,8,8,192]{4,3,2,1,0:T(8,128)(2,1)} %param.7), channel_id=1, source_target_pairs={{1,0},{2,1},{3,2},{4,3},{5,4},{6,5},{7,6},{8,7},{9,8},{10,9},{11,1... | collective-permute-start | bytes 589832 | tf_op jit(solution)/shard_map/ppermute | solution.py:17
  57.7 1.1 %copy-start.1 = (bf16[1,10,10,10,192]{4,3,2,1,0:T(8,128)(2,1)S(1)}, bf16[1,10,10,10,192]{4,3,2,1,0:T(8,128)(2,1)}, u32[]{:S(2)}) copy-start(bf16[1,10,10,10,192]{4,3,2,1,0:T(8,128)(2,1)} %maximum_maximum_fusion) | copy-start | bytes 1152004
  66.9 17.0 %collective-permute-start.2 = (bf16[1,8,8,8,192]{4,3,2,1,0:T(8,128)(2,1)S(1)}, bf16[1,8,8,8,192]{4,3,2,1,0:T(8,128)(2,1)S(1)}, u32[]{:S(2)}, u32[]{:S(2)}) collective-permute-start(bf16[1,8,8,8,192]{4,3,2,1,0:T(8,128)(2,1)S(1)} %fusion.7), channel_id=1, source_target_pairs={{0,1},{1,2},{2,3},{3,4},{4,5},{5,6},{6,7},{7,8},{8,9},{9,10},{10,1... | collective-permute-start | bytes 589832 | tf_op jit(solution)/shard_map/ppermute | solution.py:16
  76.0 13.4 %collective-permute-start.3 = (bf16[1,8,8,8,192]{4,3,2,1,0:T(8,128)(2,1)S(1)}, bf16[1,8,8,8,192]{4,3,2,1,0:T(8,128)(2,1)}, u32[]{:S(2)}, u32[]{:S(2)}) collective-permute-start(bf16[1,8,8,8,192]{4,3,2,1,0:T(8,128)(2,1)S(1)} %fusion.7), channel_id=1, source_target_pairs={{1,0},{2,1},{3,2},{4,3},{5,4},{6,5},{7,6},{8,7},{9,8},{10,9},{11,1... | collective-permute-start | bytes 589832 | tf_op jit(solution)/shard_map/ppermute | solution.py:17
Sparse Core Ops, SparseCore 0:
  9.4 20.7 all-gather.2
  32.3 19.7 all-gather.4
where the time goes:
time: 108 us
  between operations  48.5 us (45%)
  starting transfers between devices  18 us (17%)
  matrix products  16 us (15%)
  local copies, waits for them, and re-layouts  13.6 us (13%)
  waiting for transfers between devices  6.27 us (6%)
  other arithmetic  5.28 us (5%)
    conv_general_dilated x2, matrix products, conv_taps(): lax.conv_general_dilated(padded, kernel, (1, 1, 1), 'VALID', dimension_nu...  16 us
    ppermute x2, starting transfers between devices, extended(): before = lax.ppermute(last, axis, up)  14 us
    reshape x4, local copies, waits for them, and re-layouts, unpack_kernel(): grouped = stored.reshape(3, 3, 3, quarter, groups, width)  11.4 us
    ppermute x2, waiting for transfers between devices, extended(): after = lax.ppermute(leading, axis, down)  5.52 us
    ppermute x2, starting transfers between devices, extended(): after = lax.ppermute(leading, axis, down)  4.02 us
    concatenate x2, other arithmetic, pad_blocks(): return jnp.concatenate(planes, axis=1)  2.25 us
  transfers between devices with their start and end apart: 6, of which 1 were waited for; matrix products, arithmetic and copies ran while one was open for 21% of the time, Pallas kernels for 0%

commit v1 on v0

v1 whole, which is shorter than its diff:
```python
import functools

import jax
import jax.numpy as jnp
from jax import lax
from jax.experimental import pallas as pl
from jax.experimental.pallas import tpu as pltpu
from jax.sharding import PartitionSpec as P

C = 192
MESH = pl.DeviceIdType.MESH
F32 = jnp.float32
BF16 = jnp.bfloat16


def kernel(
    total, feat, occ, nbr, wk1, wk2, out,
    fsrc, hsrc, wbuf1, wbuf2, wfull, cols, tab, occs,
    lsem, fsend, frecv, wsend, wrecv, hsend, hrecv,
):
    space = lax.axis_index("space")
    core = lax.axis_index("wt")
    me = space * 2 + core
    after = me + 1
    before = me - 1
    has_after = after < total
    has_before = before >= 0
    after_id = (after // 2, after % 2)
    before_id = (lax.max(before, 0) // 2, lax.max(before, 0) % 2)
    mate_id = (space, 1 - core)

    local = [
        pltpu.make_async_copy(feat, fsrc.at[2], lsem.at[0]),
        pltpu.make_async_copy(nbr, tab, lsem.at[1]),
        pltpu.make_async_copy(occ, occs, lsem.at[2]),
        pltpu.make_async_copy(wk1, wbuf1.at[core], lsem.at[3]),
        pltpu.make_async_copy(wk2, wbuf2.at[core], lsem.at[4]),
    ]
    for copy in local:
        copy.start()

    barrier = pltpu.get_barrier_semaphore()

    @pl.when(has_after)
    def _():
        pl.semaphore_signal(barrier, inc=1, device_id=after_id, device_id_type=MESH)

    @pl.when(has_before)
    def _():
        pl.semaphore_signal(barrier, inc=1, device_id=before_id, device_id_type=MESH)

    fsrc[0] = jnp.zeros((8, 64, C), BF16)
    hsrc[0] = jnp.zeros((8, 64, C), BF16)

    pl.semaphore_wait(barrier, has_after.astype(jnp.int32) + has_before.astype(jnp.int32))

    def to_after(source, target, sems, recvs, i):
        return pltpu.make_async_remote_copy(
            src_ref=source, dst_ref=target, send_sem=sems.at[0, i], recv_sem=recvs.at[0, i],
            device_id=after_id, device_id_type=MESH)

    def to_before(source, target, sems, recvs, i):
        return pltpu.make_async_remote_copy(
            src_ref=source, dst_ref=target, send_sem=sems.at[1, i], recv_sem=recvs.at[1, i],
            device_id=before_id, device_id_type=MESH)

    fa = to_after(feat, fsrc.at[1], fsend, frecv, 0)
    fb = to_before(feat, fsrc.at[3], fsend, frecv, 0)
    pl.when(has_after)(fa.start)
    pl.when(has_before)(fb.start)

    wcopies = []
    for layer, (wk, wbuf) in enumerate(((wk1, wbuf1), (wk2, wbuf2))):
        for i in range(3):
            wcopies.append(pltpu.make_async_remote_copy(
                src_ref=wk.at[i], dst_ref=wbuf.at[core, i],
                send_sem=wsend.at[layer, i], recv_sem=wrecv.at[layer, i],
                device_id=mate_id, device_id_type=MESH))
    for copy in wcopies:
        copy.start()

    local[1].wait()
    local[2].wait()
    where = [None] * 27
    for t in range(27):
        n = tab[0, t]
        where[t] = jnp.where(n >= 0, jnp.clip(n - me + 2, 1, 3), 0)
    active = occs[0].astype(F32)

    zi = lax.broadcasted_iota(jnp.int32, (80, C), 0) % 8

    def build(src):
        def plane(X, a, xp):
            def line(c):
                def at(b):
                    t = 9 * (a + 1) + 3 * (b + 1) + (c + 1)
                    return 2 if t == 13 else where[t]
                return jnp.concatenate([
                    src[at(-1), xp, 56:64, :].astype(F32),
                    src[at(0), xp].astype(F32),
                    src[at(1), xp, 0:8, :].astype(F32),
                ], axis=0)
            left, mid, right = line(-1), line(0), line(1)
            lo = jnp.where(zi == 7, left, mid).reshape(10, 8, C)
            hi = jnp.where(zi == 0, right, mid).reshape(10, 8, C)
            shifted = (
                pltpu.roll(lo, 1, 1).reshape(80, C),
                mid,
                pltpu.roll(hi, 7, 1).reshape(80, C),
            )
            for k in range(3):
                for j in range(3):
                    cols[X, :, (3 * j + k) * C:(3 * j + k + 1) * C] = (
                        shifted[k][8 * j:8 * j + 64].astype(BF16))

        plane(0, -1, 7)
        plane(9, 1, 0)

        @pl.loop(0, 8)
        def _(x):
            plane(x + 1, 0, x)

    def unpack(wbuf, h, i):
        for jk in range(9):
            tile = wbuf[h, i, jk // 3, jk % 3]
            base = jk * C + h * 96
            base = pl.multiple_of(base, 16)
            wfull[i, pl.ds(base, 48), :] = tile[:, 0:C]
            wfull[i, pl.ds(pl.multiple_of(base + 48, 16), 48), :] = tile[:, C:2 * C]

    def conv_half(m):
        acc = None
        for i in range(3):
            lhs = cols[4 * m + i:4 * m + i + 4].reshape(256, 9 * C)
            d = jnp.dot(lhs, wfull[i], preferred_element_type=F32)
            acc = d if acc is None else acc + d
        return acc

    mate = 1 - core
    local[3].wait()
    for i in range(3):
        unpack(wbuf1, core, i)
    for i in range(3):
        wcopies[i].wait_recv()
        unpack(wbuf1, mate, i)

    local[0].wait()
    pl.when(has_before)(fa.wait_recv)
    pl.when(has_after)(fb.wait_recv)
    build(fsrc)
    ha = []
    hb = []
    for m in range(2):
        acc = conv_half(m)
        h = (jnp.maximum(acc, 0.0) * active).astype(BF16)
        hsrc[2, 4 * m:4 * m + 4] = h.reshape(4, 64, C)
        part = pl.ds(4 * m, 4)
        ha.append(to_after(hsrc.at[2, part], hsrc.at[1, part], hsend, hrecv, m))
        hb.append(to_before(hsrc.at[2, part], hsrc.at[3, part], hsend, hrecv, m))
        pl.when(has_after)(ha[m].start)
        pl.when(has_before)(hb[m].start)

    local[4].wait()
    for i in range(3):
        unpack(wbuf2, core, i)
    for i in range(3):
        wcopies[3 + i].wait_recv()
        unpack(wbuf2, mate, i)
    for m in range(2):
        pl.when(has_before)(ha[m].wait_recv)
        pl.when(has_after)(hb[m].wait_recv)
    build(hsrc)
    for m in range(2):
        acc = conv_half(m)
        res = fsrc[2, 4 * m:4 * m + 4].reshape(256, C).astype(F32)
        o = jnp.maximum(res + acc, 0.0) * active
        out[4 * m:4 * m + 4] = o.reshape(4, 64, C)

    for copy in wcopies:
        copy.wait_send()
    pl.when(has_after)(fa.wait_send)
    pl.when(has_before)(fb.wait_send)
    for m in range(2):
        pl.when(has_after)(ha[m].wait_send)
        pl.when(has_before)(hb[m].wait_send)


def body(features, occupancy, neighbours, kernel_one, kernel_two):
    total = lax.axis_size("space") * lax.axis_size("wt")
    hbm = pl.BlockSpec(memory_space=pl.ANY)
    y = pl.pallas_call(
        functools.partial(kernel, total),
        out_shape=jax.ShapeDtypeStruct((8, 64, C), F32),
        in_specs=[hbm] * 5,
        out_specs=pl.BlockSpec(memory_space=pltpu.VMEM),
        scratch_shapes=[
            pltpu.VMEM((4, 8, 64, C), BF16),
            pltpu.VMEM((4, 8, 64, C), BF16),
            pltpu.VMEM((2, 3, 3, 3, 48, 2 * C), BF16),
            pltpu.VMEM((2, 3, 3, 3, 48, 2 * C), BF16),
            pltpu.VMEM((3, 9 * C, C), BF16),
            pltpu.VMEM((10, 64, 9 * C), BF16),
            pltpu.SMEM((1, 27), jnp.int32),
            pltpu.SMEM((1,), jnp.int32),
            pltpu.SemaphoreType.DMA((5,)),
            pltpu.SemaphoreType.DMA((2, 1)),
            pltpu.SemaphoreType.DMA((2, 1)),
            pltpu.SemaphoreType.DMA((2, 3)),
            pltpu.SemaphoreType.DMA((2, 3)),
            pltpu.SemaphoreType.DMA((2, 2)),
            pltpu.SemaphoreType.DMA((2, 2)),
        ],
        compiler_params=pltpu.CompilerParams(
            collective_id=0, has_side_effects=True, vmem_limit_bytes=60 * 1024 * 1024),
    )(features.reshape(8, 64, C), occupancy, neighbours, kernel_one, kernel_two)
    return y.reshape(1, 8, 8, 8, C)


def solution(mesh):
    return jax.shard_map(
        body,
        mesh=mesh,
        in_specs=(
            P(("space", "wt"), None, None, None, None),
            P(("space", "wt")),
            P(("space", "wt"), None),
            P(None, None, None, None, "wt"),
            P(None, None, None, None, "wt"),
        ),
        out_specs=P(("space", "wt"), None, None, None, None),
        check_vma=False,
    )
```

time: 108 us -> 29.5 us (0.27)
  the two profiles are of different devices: /device:TPU:255 before, /device:TPU:256 now
where the time goes in v1:
time: 29.5 us; the launch traced here: 29.3 us
  Pallas kernels  26.7 us (91%)
  local copies, waits for them, and re-layouts  1.87 us (6%)
  between operations  0.66 us (2%)
    pallas_call x1, Pallas kernels, body(): pl.pallas_call(functools.partial(kernel, total), out_shape=jax.ShapeDtype...  26.7 us
    unnamed x1, local copies, waits for them, and re-layouts  1.87 us

profile of v1, /device:TPU:256, one launch (start us, length us, event | category | flops | bytes accessed | tf_op | source)
XLA Modules:
  0.0 29.3 jit_solution(3529952885715831313)
XLA Ops:
  0.7 26.7 %shard_map.55 = f32[8,64,192]{2,1,0:T(8,128)} custom-call(bf16[8,64,192]{2,1,0:T(8,128)(2,1)} %bitcast.3, s32[1]{0:T(128)S(6)} %copy.7.occ, s32[1,27]{1,0:T(1,128)} %nbr.1, bf16[3,3,3,48,384]{4,3,2,1,0:T(8,128)(2,1)} %wk1.1, bf16[3,3,3,48,384]{4,3,2,1,0:T(8,128)(2,1)} %wk2.1), custom_call_target="tpu_custom_call" | custom-call | tf_op jit(solution)/shard_map/pallas_call | solution.py:191
  27.4 1.9 %copy.8 = f32[1,8,8,8,192]{4,3,2,1,0:T(8,128)} copy(f32[1,8,8,8,192]{4,3,2,1,0:T(8,128)} %bitcast.2) | data formatting | bytes 786432

commit v2 on v0

v2 whole, which is shorter than its diff:
```python
import functools

import jax
import jax.numpy as jnp
from jax import lax
from jax.experimental import pallas as pl
from jax.experimental.pallas import tpu as pltpu
from jax.sharding import PartitionSpec as P

C = 192
MESH = pl.DeviceIdType.MESH
F32 = jnp.float32
BF16 = jnp.bfloat16
FACES = ((-1, 0, 0), (1, 0, 0), (0, -1, 0), (0, 1, 0), (0, 0, -1), (0, 0, 1))


def columns(dst, low, mid, high):
    row = lax.broadcasted_iota(jnp.int32, (80, C), 0) % 8
    lo = jnp.where(row == 7, low, mid).reshape(10, 8, C)
    hi = jnp.where(row == 0, high, mid).reshape(10, 8, C)
    shifted = (pltpu.roll(lo, 1, 1).reshape(80, C), mid, pltpu.roll(hi, 7, 1).reshape(80, C))
    for inner in range(3):
        for outer in range(3):
            at = (3 * outer + inner) * C
            dst[:, at:at + C] = shifted[inner][8 * outer:8 * outer + 64].astype(BF16)


def framed(value):
    edge = jnp.zeros((8, C), F32)
    return jnp.concatenate([edge, value, edge], axis=0)


def own_columns(cols, src):
    @pl.loop(0, 8)
    def _(x):
        columns(cols.at[x + 1], 0.0, framed(src[x].astype(F32)), 0.0)


def own_conv(cols, weights, half):
    acc = None
    for i in range(3):
        lhs = cols[4 * half + i:4 * half + i + 4].reshape(256, 9 * C)
        d = jnp.dot(lhs, weights[i], preferred_element_type=F32)
        acc = d if acc is None else acc + d
    return acc


def face_columns(dst, surf, where):
    def at(a, b, c):
        return where[9 * (a + 1) + 3 * (b + 1) + (c + 1)]

    def face(source, axis, side):
        pair = surf[source, axis]
        return (pair[:, C:] if side < 0 else pair[:, :C]).astype(F32)

    for n, (a, b, c) in enumerate(FACES):
        if a:
            def line(v):
                return jnp.concatenate([
                    face(at(a, -1, v), 0, a)[56:64],
                    face(at(a, 0, v), 0, a),
                    face(at(a, 1, v), 0, a)[0:8],
                ], axis=0)
            columns(dst.at[n], line(-1), line(0), line(1))
        elif b:
            columns(dst.at[n], *(framed(face(at(0, b, v), 1, b)) for v in (-1, 0, 1)))
        else:
            columns(dst.at[n], 0.0, framed(face(at(0, 0, c), 2, c)), 0.0)


def face_product(fcols, weights, n):
    a, b, c = FACES[n]
    if a:
        rhs = weights[a + 1]
    elif b:
        at = 3 * C * (b + 1)
        rhs = jnp.concatenate([weights[i, at:at + 3 * C] for i in range(3)], axis=0)
    else:
        rhs = jnp.concatenate(
            [weights[i, (3 * j + c + 1) * C:(3 * j + c + 2) * C] for i in range(3) for j in range(3)], axis=0)
    return jnp.dot(fcols[n], rhs, preferred_element_type=F32)


def put(acc, rows, value):
    acc[0, rows, :] = value[:, :128]
    acc[1, rows, 0:C - 128] = value[:, 128:]


def get(acc, rows):
    return jnp.concatenate([acc[0, rows, :], acc[1, rows, 0:C - 128]], axis=1)


def add_faces(acc, fcols, weights):
    for n, (a, b, c) in enumerate(FACES):
        d = face_product(fcols, weights, n)
        if a:
            rows = slice(0, 64) if a < 0 else slice(448, 512)
            put(acc, rows, get(acc, rows) + d)
        elif b:
            first = 0 if b < 0 else 56
            for x in range(8):
                rows = slice(64 * x + first, 64 * x + first + 8)
                put(acc, rows, get(acc, rows) + d[8 * x:8 * x + 8])
        else:
            rows = pl.ds(0 if c < 0 else 7, 64, stride=8)
            rest = jnp.concatenate([d[:, 128:], jnp.zeros((64, 256 - C), F32)], axis=1)
            for part, value in enumerate((d[:, :128], rest)):
                acc[part, rows, :] = acc[part, rows, :] + value


def pack_faces(dst, field, fix):
    def strided(first):
        rows = pl.ds(first, 64, stride=8)
        return jnp.concatenate([field[0, rows, :], field[1, rows, :][:, 0:C - 128]], axis=1)

    dst[0, :, :C] = fix(get(field, slice(0, 64)))
    dst[0, :, C:] = fix(get(field, slice(448, 512)))
    for side, first in enumerate((0, 56)):
        rows = jnp.concatenate(
            [get(field, slice(64 * x + first, 64 * x + first + 8)) for x in range(8)], axis=0)
        dst[1, :, side * C:(side + 1) * C] = fix(rows)
    dst[2, :, :C] = fix(strided(0))
    dst[2, :, C:] = fix(strided(7))


def exchange_kernel(
    total, feat, occ, nbr, wk1, wk2,
    hcols, w2, acc2, act,
    own, fsurf, hsurf, wbuf1, wbuf2, w1, cols, fcols, acc, tab, occs,
    lsem, fsend, frecv, wsend, wrecv, hsend, hrecv,
):
    space = lax.axis_index("space")
    core = lax.axis_index("wt")
    mate = 1 - core
    me = space * 2 + core
    after = me + 1
    before = me - 1
    has_after = after < total
    has_before = before >= 0
    after_id = (after // 2, after % 2)
    before_id = (lax.max(before, 0) // 2, lax.max(before, 0) % 2)

    barrier = pltpu.get_barrier_semaphore()

    @pl.when(has_after)
    def _():
        pl.semaphore_signal(barrier, inc=1, device_id=after_id, device_id_type=MESH)

    @pl.when(has_before)
    def _():
        pl.semaphore_signal(barrier, inc=1, device_id=before_id, device_id_type=MESH)

    local = [
        pltpu.make_async_copy(feat, own, lsem.at[0]),
        pltpu.make_async_copy(nbr, tab, lsem.at[1]),
        pltpu.make_async_copy(occ, occs, lsem.at[2]),
        pltpu.make_async_copy(wk1, wbuf1.at[core], lsem.at[3]),
        pltpu.make_async_copy(wk2, wbuf2.at[core], lsem.at[4]),
    ]
    for copy in local:
        copy.start()

    fsurf[0] = jnp.zeros((3, 64, 2 * C), BF16)
    hsurf[0] = jnp.zeros((3, 64, 2 * C), BF16)
    cols[0] = jnp.zeros((64, 9 * C), BF16)
    cols[9] = jnp.zeros((64, 9 * C), BF16)

    local[0].wait()
    for x in range(8):
        put(acc, slice(64 * x, 64 * x + 64), own[x].astype(F32))
    pack_faces(fsurf.at[2], acc, lambda v: v.astype(BF16))

    pl.semaphore_wait(barrier, has_after.astype(jnp.int32) + has_before.astype(jnp.int32))

    def sends(surf, sems, recvs):
        ahead = pltpu.make_async_remote_copy(
            src_ref=surf.at[2], dst_ref=surf.at[1], send_sem=sems.at[0], recv_sem=recvs.at[0],
            device_id=after_id, device_id_type=MESH)
        back = pltpu.make_async_remote_copy(
            src_ref=surf.at[2], dst_ref=surf.at[3], send_sem=sems.at[1], recv_sem=recvs.at[1],
            device_id=before_id, device_id_type=MESH)
        return ahead, back

    fa, fb = sends(fsurf, fsend, frecv)
    pl.when(has_after)(fa.start)
    pl.when(has_before)(fb.start)
    wcopies = [
        pltpu.make_async_remote_copy(
            src_ref=wk, dst_ref=wbuf.at[core], send_sem=wsend.at[n], recv_sem=wrecv.at[n],
            device_id=(space, mate), device_id_type=MESH)
        for n, (wk, wbuf) in enumerate(((wk1, wbuf1), (wk2, wbuf2)))
    ]
    for copy in wcopies:
        copy.start()

    local[1].wait()
    local[2].wait()
    where = []
    for t in range(27):
        n = tab[0, t]
        where.append(jnp.where(n >= 0, jnp.clip(n - me + 2, 1, 3), 0))
    active = occs[0].astype(F32)

    def unpack(wbuf, weights, h):
        base = pl.multiple_of(h * 96, 16)

        @pl.loop(0, 3)
        def _(i):
            for jk in range(9):
                tile = wbuf[h, i, jk // 3, jk % 3]
                weights[i, pl.ds(base + jk * C, 48), :] = tile[:, 0:C]
                weights[i, pl.ds(base + jk * C + 48, 48), :] = tile[:, C:2 * C]

    own_columns(cols, own)
    local[3].wait()
    unpack(wbuf1, w1, core)
    wcopies[0].wait_recv()
    unpack(wbuf1, w1, mate)
    for half in range(2):
        put(acc, slice(256 * half, 256 * half + 256), own_conv(cols, w1, half))
    local[4].wait()
    unpack(wbuf2, w2, core)
    wcopies[1].wait_recv()
    unpack(wbuf2, w2, mate)

    pl.when(has_before)(fa.wait_recv)
    pl.when(has_after)(fb.wait_recv)
    face_columns(fcols, fsurf, where)
    add_faces(acc, fcols, w1)

    def hidden(v):
        return (jnp.maximum(v, 0.0) * active).astype(BF16)

    pack_faces(hsurf.at[2], acc, hidden)
    ha, hb = sends(hsurf, hsend, hrecv)
    pl.when(has_after)(ha.start)
    pl.when(has_before)(hb.start)

    @pl.loop(0, 8)
    def _(x):
        v = hidden(get(acc, pl.ds(pl.multiple_of(64 * x, 64), 64)))
        columns(cols.at[x + 1], 0.0, framed(v.astype(F32)), 0.0)

    for half in range(2):
        res = own[4 * half:4 * half + 4].reshape(256, C).astype(F32)
        put(acc2, slice(256 * half, 256 * half + 256), res + own_conv(cols, w2, half))
    act[...] = jnp.full((8, C), active, F32)

    for copy in wcopies:
        copy.wait_send()
    pl.when(has_after)(fa.wait_send)
    pl.when(has_before)(fb.wait_send)
    pl.when(has_before)(ha.wait_recv)
    pl.when(has_after)(hb.wait_recv)
    face_columns(hcols, hsurf, where)
    pl.when(has_after)(ha.wait_send)
    pl.when(has_before)(hb.wait_send)


def finish_kernel(hcols, w2, acc2, act, out, acc):
    acc[...] = acc2[...]
    add_faces(acc, hcols, w2)
    scale = act[0:1, :]
    for x in range(8):
        v = jnp.maximum(get(acc, slice(64 * x, 64 * x + 64)), 0.0) * scale
        out[x] = v


def body(features, occupancy, neighbours, kernel_one, kernel_two):
    total = lax.axis_size("space") * lax.axis_size("wt")
    hbm = pl.BlockSpec(memory_space=pltpu.HBM)
    vmem = pl.BlockSpec(memory_space=pltpu.VMEM)

    def pinned(v):
        return pltpu.with_memory_space_constraint(v, pltpu.HBM)

    middle = pl.pallas_call(
        functools.partial(exchange_kernel, total),
        out_shape=(
            pltpu.VMEM((6, 64, 9 * C), BF16),
            pltpu.VMEM((3, 9 * C, C), BF16),
            pltpu.VMEM((2, 512, 128), F32),
            pltpu.VMEM((8, C), F32),
        ),
        in_specs=[hbm] * 5,
        out_specs=(vmem,) * 4,
        scratch_shapes=[
            pltpu.VMEM((8, 64, C), BF16),
            pltpu.VMEM((4, 3, 64, 2 * C), BF16),
            pltpu.VMEM((4, 3, 64, 2 * C), BF16),
            pltpu.VMEM((2, 3, 3, 3, 48, 2 * C), BF16),
            pltpu.VMEM((2, 3, 3, 3, 48, 2 * C), BF16),
            pltpu.VMEM((3, 9 * C, C), BF16),
            pltpu.VMEM((10, 64, 9 * C), BF16),
            pltpu.VMEM((6, 64, 9 * C), BF16),
            pltpu.VMEM((2, 512, 128), F32),
            pltpu.SMEM((1, 27), jnp.int32),
            pltpu.SMEM((1,), jnp.int32),
            pltpu.SemaphoreType.DMA((5,)),
            pltpu.SemaphoreType.DMA((2,)),
            pltpu.SemaphoreType.DMA((2,)),
            pltpu.SemaphoreType.DMA((2,)),
            pltpu.SemaphoreType.DMA((2,)),
            pltpu.SemaphoreType.DMA((2,)),
            pltpu.SemaphoreType.DMA((2,)),
        ],
        compiler_params=pltpu.CompilerParams(
            collective_id=0, has_side_effects=True, vmem_limit_bytes=32 * 1024 * 1024),
    )(pinned(features.reshape(8, 64, C)), occupancy, pinned(neighbours), pinned(kernel_one), pinned(kernel_two))
    y = pl.pallas_call(
        finish_kernel,
        out_shape=jax.ShapeDtypeStruct((8, 64, C), F32),
        in_specs=[vmem] * 4,
        out_specs=vmem,
        scratch_shapes=[pltpu.VMEM((2, 512, 128), F32)],
        compiler_params=pltpu.CompilerParams(vmem_limit_bytes=16 * 1024 * 1024),
    )(*middle)
    return y.reshape(1, 8, 8, 8, C)


def solution(mesh):
    return jax.shard_map(
        body,
        mesh=mesh,
        in_specs=(
            P(("space", "wt"), None, None, None, None),
            P(("space", "wt")),
            P(("space", "wt"), None),
            P(None, None, None, None, "wt"),
            P(None, None, None, None, "wt"),
        ),
        out_specs=P(("space", "wt"), None, None, None, None),
        check_vma=False,
    )
```

time: 108 us -> 22.4 us (0.21)
  the two profiles are of different devices: /device:TPU:255 before, /device:TPU:256 now
where the time goes in v2:
time: 22.4 us; the launch traced here: 22.3 us
  Pallas kernels  21.6 us (96%)
  between operations  0.66 us (3%)
    pallas_call x1, Pallas kernels, body(): pl.pallas_call(functools.partial(exchange_kernel, total), out_shape=(pltp...  19.7 us
    pallas_call x1, Pallas kernels, body(): pl.pallas_call(finish_kernel, out_shape=jax.ShapeDtypeStruct((8, 64, C),...  1.89 us

profile of v2, /device:TPU:256, one launch (start us, length us, event | category | flops | bytes accessed | tf_op | source)
XLA Modules:
  0.0 22.3 jit_solution(961693719115612867)
XLA Ops:
  0.7 19.7 %shard_map.55 = (bf16[6,64,1728]{2,1,0:T(8,128)(2,1)S(1)}, bf16[3,1728,192]{2,1,0:T(8,128)(2,1)S(1)}, f32[2,512,128]{2,1,0:T(8,128)S(1)}, f32[8,192]{1,0:T(8,128)S(1)}) custom-call(bf16[8,64,192]{2,1,0:T(8,128)(2,1)} %bitcast.2, s32[1]{0:T(128)S(6)} %copy.6.occ, s32[1,27]{1,0:T(1,128)} %nbr.1, bf16[3,3,3,48,384]{4,3,2,1,0:T(8,128)(2,1)} %wk1.1, ...), custom_call_target="tpu_custom_call" | custom-call | tf_op jit(solution)/shard_map/pallas_call | solution.py:277
  20.4 1.9 %shard_map.56 = f32[8,64,192]{2,1,0:T(8,128)} custom-call(bf16[6,64,1728]{2,1,0:T(8,128)(2,1)S(1)} %get-tuple-element.9.hcols, bf16[3,1728,192]{2,1,0:T(8,128)(2,1)S(1)} %get-tuple-element.10.w2, f32[2,512,128]{2,1,0:T(8,128)S(1)} %get-tuple-element.11.acc2, f32[8,192]{1,0:T(8,128)S(1)} %get-tuple-element.12.act), custom_call_target="tpu_custom_call" | custom-call | tf_op jit(solution)/shard_map/pallas_call | solution.py:310

commit v3 on v2

v3 whole, which is shorter than its diff:
```python
import functools

import jax
import jax.numpy as jnp
from jax import lax
from jax.experimental import pallas as pl
from jax.experimental.pallas import tpu as pltpu
from jax.sharding import PartitionSpec as P

C = 192
MESH = pl.DeviceIdType.MESH
F32 = jnp.float32
BF16 = jnp.bfloat16
FACES = ((-1, 0, 0), (1, 0, 0), (0, -1, 0), (0, 1, 0), (0, 0, -1), (0, 0, 1))


def columns(dst, low, mid, high):
    row = lax.broadcasted_iota(jnp.int32, (80, C), 0) % 8
    lo = jnp.where(row == 7, low, mid).reshape(10, 8, C)
    hi = jnp.where(row == 0, high, mid).reshape(10, 8, C)
    shifted = (pltpu.roll(lo, 1, 1).reshape(80, C), mid, pltpu.roll(hi, 7, 1).reshape(80, C))
    for inner in range(3):
        for outer in range(3):
            at = (3 * outer + inner) * C
            dst[:, at:at + C] = shifted[inner][8 * outer:8 * outer + 64].astype(BF16)


def framed(value):
    edge = jnp.zeros((8, C), F32)
    return jnp.concatenate([edge, value, edge], axis=0)


def own_columns(cols, src):
    @pl.loop(0, 8)
    def _(x):
        columns(cols.at[x + 1], 0.0, framed(src[x].astype(F32)), 0.0)


def taps(weights, chosen):
    return jnp.concatenate([weights[h, t] for t in chosen for h in range(2)], axis=0)


def own_conv(cols, weights, half):
    acc = None
    for i in range(3):
        lhs = cols[4 * half + i:4 * half + i + 4].reshape(256, 9 * C)
        d = jnp.dot(lhs, taps(weights, range(9 * i, 9 * i + 9)), preferred_element_type=F32)
        acc = d if acc is None else acc + d
    return acc


def face_columns(dst, surf, where, n):
    a, b, c = FACES[n]

    def face(p, q, r):
        pair = surf[where[9 * (p + 1) + 3 * (q + 1) + (r + 1)]]
        return (pair[:, C:] if a + b + c < 0 else pair[:, :C]).astype(F32)

    if a:
        def line(r):
            return jnp.concatenate([face(a, -1, r)[56:64], face(a, 0, r), face(a, 1, r)[0:8]], axis=0)
        columns(dst.at[n], line(-1), line(0), line(1))
    elif b:
        columns(dst.at[n], *(framed(face(0, b, r)) for r in (-1, 0, 1)))
    else:
        columns(dst.at[n], 0.0, framed(face(0, 0, c)), 0.0)


def face_product(fcols, weights, n):
    a, b, c = FACES[n]
    if a:
        chosen = [9 * (a + 1) + t for t in range(9)]
    elif b:
        chosen = [9 * i + 3 * (b + 1) + k for i in range(3) for k in range(3)]
    else:
        chosen = [9 * i + 3 * j + c + 1 for i in range(3) for j in range(3)]
    return jnp.dot(fcols[n], taps(weights, chosen), preferred_element_type=F32)


def put(acc, rows, value):
    acc[0, rows, :] = value[:, :128]
    acc[1, rows, 0:C - 128] = value[:, 128:]


def get(acc, rows):
    return jnp.concatenate([acc[0, rows, :], acc[1, rows, 0:C - 128]], axis=1)


def add_pair(acc, fcols, surf, where, weights, axis):
    for n in (2 * axis, 2 * axis + 1):
        face_columns(fcols, surf, where, n)
    for n in (2 * axis, 2 * axis + 1):
        a, b, c = FACES[n]
        d = face_product(fcols, weights, n)
        if a:
            rows = slice(0, 64) if a < 0 else slice(448, 512)
            put(acc, rows, get(acc, rows) + d)
        elif b:
            first = 0 if b < 0 else 56
            for x in range(8):
                rows = slice(64 * x + first, 64 * x + first + 8)
                put(acc, rows, get(acc, rows) + d[8 * x:8 * x + 8])
        else:
            rows = pl.ds(0 if c < 0 else 7, 64, stride=8)
            rest = jnp.concatenate([d[:, 128:], jnp.zeros((64, 256 - C), F32)], axis=1)
            for part, value in enumerate((d[:, :128], rest)):
                acc[part, rows, :] = acc[part, rows, :] + value


def pack_pair(dst, field, fix, axis):
    def rows_of(side):
        if axis == 0:
            return get(field, slice(448 * side, 448 * side + 64))
        if axis == 1:
            return jnp.concatenate(
                [get(field, slice(64 * x + 56 * side, 64 * x + 56 * side + 8)) for x in range(8)], axis=0)
        rows = pl.ds(7 * side, 64, stride=8)
        return jnp.concatenate([field[0, rows, :], field[1, rows, :][:, 0:C - 128]], axis=1)

    dst[:, :C] = fix(rows_of(0))
    dst[:, C:] = fix(rows_of(1))


def exchange_kernel(
    total, feat, occ, nbr, wk1, wk2,
    acc2, act,
    own, fx, fy, fz, hx, hy, hz, stage1, stage2, w1, w2, cols, fcols, acc, tab, occs,
    lsem, fsend, frecv, wsend, wrecv, hsend, hrecv,
):
    space = lax.axis_index("space")
    core = lax.axis_index("wt")
    mate = 1 - core
    fsurf = (fx, fy, fz)
    hsurf = (hx, hy, hz)
    me = space * 2 + core
    after = me + 1
    before = me - 1
    has_after = after < total
    has_before = before >= 0
    after_id = (after // 2, after % 2)
    before_id = (lax.max(before, 0) // 2, lax.max(before, 0) % 2)

    barrier = pltpu.get_barrier_semaphore()

    @pl.when(has_after)
    def _():
        pl.semaphore_signal(barrier, inc=1, device_id=after_id, device_id_type=MESH)

    @pl.when(has_before)
    def _():
        pl.semaphore_signal(barrier, inc=1, device_id=before_id, device_id_type=MESH)

    local = [
        pltpu.make_async_copy(feat, own, lsem.at[0]),
        pltpu.make_async_copy(nbr, tab, lsem.at[1]),
        pltpu.make_async_copy(occ, occs, lsem.at[2]),
        pltpu.make_async_copy(wk1, stage1, lsem.at[3]),
        pltpu.make_async_copy(wk2, stage2, lsem.at[4]),
    ]
    for copy in local:
        copy.start()

    for surf in fsurf + hsurf:
        surf[0] = jnp.zeros((64, 2 * C), BF16)
    cols[0] = jnp.zeros((64, 9 * C), BF16)
    cols[9] = jnp.zeros((64, 9 * C), BF16)

    local[0].wait()
    for x in range(8):
        put(acc, slice(64 * x, 64 * x + 64), own[x].astype(F32))
    for axis in range(3):
        pack_pair(fsurf[axis].at[2], acc, lambda v: v.astype(BF16), axis)

    def unpack(stage, weights):
        @pl.loop(0, 3)
        def _(i):
            for jk in range(9):
                tile = stage[i, jk // 3, jk % 3]
                weights[core, 9 * i + jk, 0:48, :] = tile[:, 0:C]
                weights[core, 9 * i + jk, 48:96, :] = tile[:, C:2 * C]

    local[3].wait()
    unpack(stage1, w1)

    pl.semaphore_wait(barrier, has_after.astype(jnp.int32) + has_before.astype(jnp.int32))

    def sends(surf, sems, recvs, axis):
        ahead = pltpu.make_async_remote_copy(
            src_ref=surf[axis].at[2], dst_ref=surf[axis].at[1],
            send_sem=sems.at[0, axis], recv_sem=recvs.at[0, axis],
            device_id=after_id, device_id_type=MESH)
        back = pltpu.make_async_remote_copy(
            src_ref=surf[axis].at[2], dst_ref=surf[axis].at[3],
            send_sem=sems.at[1, axis], recv_sem=recvs.at[1, axis],
            device_id=before_id, device_id_type=MESH)
        return ahead, back

    fcopies = [sends(fsurf, fsend, frecv, axis) for axis in range(3)]
    hcopies = [sends(hsurf, hsend, hrecv, axis) for axis in range(3)]

    def start(pair):
        pl.when(has_after)(pair[0].start)
        pl.when(has_before)(pair[1].start)

    def received(pair):
        pl.when(has_before)(pair[0].wait_recv)
        pl.when(has_after)(pair[1].wait_recv)

    def sent(pair):
        pl.when(has_after)(pair[0].wait_send)
        pl.when(has_before)(pair[1].wait_send)

    wcopies = [
        pltpu.make_async_remote_copy(
            src_ref=w.at[core], dst_ref=w.at[core], send_sem=wsend.at[n], recv_sem=wrecv.at[n],
            device_id=(space, mate), device_id_type=MESH)
        for n, w in enumerate((w1, w2))
    ]
    for pair in fcopies:
        start(pair)
    wcopies[0].start()

    local[1].wait()
    local[2].wait()
    where = []
    for t in range(27):
        n = tab[0, t]
        where.append(jnp.where(n >= 0, jnp.clip(n - me + 2, 1, 3), 0))
    active = occs[0].astype(F32)

    own_columns(cols, own)
    local[4].wait()
    unpack(stage2, w2)
    wcopies[1].start()
    wcopies[0].wait_recv()
    for half in range(2):
        put(acc, slice(256 * half, 256 * half + 256), own_conv(cols, w1, half))
    for axis in range(3):
        received(fcopies[axis])
        add_pair(acc, fcols, fsurf[axis], where, w1, axis)

    def hidden(v):
        return (jnp.maximum(v, 0.0) * active).astype(BF16)

    for axis in range(3):
        pack_pair(hsurf[axis].at[2], acc, hidden, axis)
        start(hcopies[axis])

    @pl.loop(0, 8)
    def _(x):
        v = hidden(get(acc, pl.ds(pl.multiple_of(64 * x, 64), 64)))
        columns(cols.at[x + 1], 0.0, framed(v.astype(F32)), 0.0)

    wcopies[1].wait_recv()
    for half in range(2):
        res = own[4 * half:4 * half + 4].reshape(256, C).astype(F32)
        put(acc2, slice(256 * half, 256 * half + 256), res + own_conv(cols, w2, half))
    act[...] = jnp.full((8, C), active, F32)

    for copy in wcopies:
        copy.wait_send()
    for pair in fcopies:
        sent(pair)
    for axis in range(3):
        received(hcopies[axis])
        add_pair(acc2, fcols, hsurf[axis], where, w2, axis)
    for pair in hcopies:
        sent(pair)


def finish_kernel(acc2, act, out, done, sem):
    scale = act[0:1, :]
    copies = []
    for part in range(4):
        for x in (2 * part, 2 * part + 1):
            done[x] = jnp.maximum(get(acc2, slice(64 * x, 64 * x + 64)), 0.0) * scale
        rows = pl.ds(2 * part, 2)
        copies.append(pltpu.make_async_copy(done.at[rows], out.at[rows], sem.at[part]))
        copies[part].start()
    for copy in copies:
        copy.wait()


def body(features, occupancy, neighbours, kernel_one, kernel_two):
    total = lax.axis_size("space") * lax.axis_size("wt")
    hbm = pl.BlockSpec(memory_space=pltpu.HBM)
    vmem = pl.BlockSpec(memory_space=pltpu.VMEM)

    def pinned(v):
        return pltpu.with_memory_space_constraint(v, pltpu.HBM)

    middle = pl.pallas_call(
        functools.partial(exchange_kernel, total),
        out_shape=(
            pltpu.VMEM((2, 512, 128), F32),
            pltpu.VMEM((8, C), F32),
        ),
        in_specs=[hbm] * 5,
        out_specs=(vmem,) * 2,
        scratch_shapes=[
            pltpu.VMEM((8, 64, C), BF16),
            *[pltpu.VMEM((4, 64, 2 * C), BF16)] * 6,
            pltpu.VMEM((3, 3, 3, 48, 2 * C), BF16),
            pltpu.VMEM((3, 3, 3, 48, 2 * C), BF16),
            pltpu.VMEM((2, 27, 96, C), BF16),
            pltpu.VMEM((2, 27, 96, C), BF16),
            pltpu.VMEM((10, 64, 9 * C), BF16),
            pltpu.VMEM((6, 64, 9 * C), BF16),
            pltpu.VMEM((2, 512, 128), F32),
            pltpu.SMEM((1, 27), jnp.int32),
            pltpu.SMEM((1,), jnp.int32),
            pltpu.SemaphoreType.DMA((5,)),
            pltpu.SemaphoreType.DMA((2, 3)),
            pltpu.SemaphoreType.DMA((2, 3)),
            pltpu.SemaphoreType.DMA((2,)),
            pltpu.SemaphoreType.DMA((2,)),
            pltpu.SemaphoreType.DMA((2, 3)),
            pltpu.SemaphoreType.DMA((2, 3)),
        ],
        compiler_params=pltpu.CompilerParams(
            collective_id=0, has_side_effects=True, vmem_limit_bytes=32 * 1024 * 1024),
    )(pinned(features.reshape(8, 64, C)), occupancy, pinned(neighbours), pinned(kernel_one), pinned(kernel_two))
    y = pl.pallas_call(
        finish_kernel,
        out_shape=jax.ShapeDtypeStruct((8, 64, C), F32),
        in_specs=[vmem] * 2,
        out_specs=hbm,
        scratch_shapes=[pltpu.VMEM((8, 64, C), F32), pltpu.SemaphoreType.DMA((4,))],
        compiler_params=pltpu.CompilerParams(vmem_limit_bytes=16 * 1024 * 1024),
    )(*middle)
    return y.reshape(1, 8, 8, 8, C)


def solution(mesh):
    return jax.shard_map(
        body,
        mesh=mesh,
        in_specs=(
            P(("space", "wt"), None, None, None, None),
            P(("space", "wt")),
            P(("space", "wt"), None),
            P(None, None, None, None, "wt"),
            P(None, None, None, None, "wt"),
        ),
        out_specs=P(("space", "wt"), None, None, None, None),
        check_vma=False,
    )
```

time: 22.4 us -> 21.8 us (0.973)
  the two profiles are of different devices: /device:TPU:256 before, /device:TPU:1 now
where the time goes in v3:
time: 21.8 us; the launch traced here: 21.7 us
  Pallas kernels  21 us (96%)
  between operations  0.66 us (3%)
    pallas_call x1, Pallas kernels, body(): pl.pallas_call(functools.partial(exchange_kernel, total), out_shape=(pltp...  20.2 us
    pallas_call x1, Pallas kernels, body(): pl.pallas_call(finish_kernel, out_shape=jax.ShapeDtypeStruct((8, 64, C),...  0.83 us

profile of v3, /device:TPU:1, one launch (start us, length us, event | category | flops | bytes accessed | tf_op | source)
XLA Modules:
  0.0 21.7 jit_solution(13121767223757825141)
XLA Ops:
  0.7 20.2 %shard_map.55 = (f32[2,512,128]{2,1,0:T(8,128)S(1)}, f32[8,192]{1,0:T(8,128)S(1)}) custom-call(bf16[8,64,192]{2,1,0:T(8,128)(2,1)} %bitcast.2, s32[1]{0:T(128)S(6)} %copy.6.occ, s32[1,27]{1,0:T(1,128)} %nbr.1, bf16[3,3,3,48,384]{4,3,2,1,0:T(8,128)(2,1)} %wk1.1, bf16[3,3,3,48,384]{4,3,2,1,0:T(8,128)(2,1)} %wk2.1), custom_call_target="tpu_custom_call" | custom-call | tf_op jit(solution)/shard_map/pallas_call | solution.py:292
  20.9 0.8 %shard_map.56 = f32[8,64,192]{2,1,0:T(8,128)} custom-call(f32[2,512,128]{2,1,0:T(8,128)S(1)} %get-tuple-element.7.acc2, f32[8,192]{1,0:T(8,128)S(1)} %get-tuple-element.8.act), custom_call_target="tpu_custom_call" | custom-call | tf_op jit(solution)/shard_map/pallas_call | solution.py:323

commit v4 on v3

--- a/solution.py
+++ b/solution.py
@@ -11,6 +11,7 @@
 MESH = pl.DeviceIdType.MESH
 F32 = jnp.float32
 BF16 = jnp.bfloat16
+ROW = 32
 FACES = ((-1, 0, 0), (1, 0, 0), (0, -1, 0), (0, 1, 0), (0, 0, -1), (0, 0, 1))
 
 
@@ -30,23 +31,17 @@
     return jnp.concatenate([edge, value, edge], axis=0)
 
 
-def own_columns(cols, src):
-    @pl.loop(0, 8)
-    def _(x):
-        columns(cols.at[x + 1], 0.0, framed(src[x].astype(F32)), 0.0)
+def own_columns(dst, value):
+    columns(dst, 0.0, framed(value.astype(F32)), 0.0)
 
 
 def taps(weights, chosen):
     return jnp.concatenate([weights[h, t] for t in chosen for h in range(2)], axis=0)
 
 
-def own_conv(cols, weights, half):
-    acc = None
-    for i in range(3):
-        lhs = cols[4 * half + i:4 * half + i + 4].reshape(256, 9 * C)
-        d = jnp.dot(lhs, taps(weights, range(9 * i, 9 * i + 9)), preferred_element_type=F32)
-        acc = d if acc is None else acc + d
-    return acc
+def own_product(cols, weights, i, first, last):
+    lhs = cols[first + i - 1:last + i - 1].reshape(64 * (last - first), 9 * C)
+    return jnp.dot(lhs, taps(weights, range(9 * i, 9 * i + 9)), preferred_element_type=F32)
 
 
 def face_columns(dst, surf, where, n):
@@ -86,9 +81,7 @@
     return jnp.concatenate([acc[0, rows, :], acc[1, rows, 0:C - 128]], axis=1)
 
 
-def add_pair(acc, fcols, surf, where, weights, axis):
-    for n in (2 * axis, 2 * axis + 1):
-        face_columns(fcols, surf, where, n)
+def add_pair(acc, fcols, weights, axis):
     for n in (2 * axis, 2 * axis + 1):
         a, b, c = FACES[n]
         d = face_product(fcols, weights, n)
@@ -107,6 +100,16 @@
                 acc[part, rows, :] = acc[part, rows, :] + value
 
 
+def add_faces(acc, fcols, surf, where, weights, arrived):
+    for axis in range(3):
+        arrived(axis)
+        if axis:
+            add_pair(acc, fcols, weights, axis - 1)
+        for n in (2 * axis, 2 * axis + 1):
+            face_columns(fcols, surf[axis], where, n)
+    add_pair(acc, fcols, weights, 2)
+
+
 def pack_pair(dst, field, fix, axis):
     def rows_of(side):
         if axis == 0:
@@ -124,31 +127,35 @@
 def exchange_kernel(
     total, feat, occ, nbr, wk1, wk2,
     acc2, act,
-    own, fx, fy, fz, hx, hy, hz, stage1, stage2, w1, w2, cols, fcols, acc, tab, occs,
-    lsem, fsend, frecv, wsend, wrecv, hsend, hrecv,
+    own, fx, fy, fz, ex, ey, ez, hx, hy, hz, stage1, stage2, w1, w2, cols, fcols, acc, facc,
+    px, py, pz, qx, qy, qz, ftab, tab, tab2, occs,
+    lsem, fsend, frecv, wsend, wrecv, hsend, hrecv, psend, precv,
 ):
     space = lax.axis_index("space")
     core = lax.axis_index("wt")
+    chips = total // 2
+    me = space * 2 + core
     mate = 1 - core
+    mate_slot = space * 2 + mate
+    step = 2 * core - 1
+    far = space + step
+    has_far = (far >= 0) & (far < chips)
+    far_id = (jnp.clip(far, 0, chips - 1), mate)
+    mate_id = (space, mate)
+    long = has_far & ((space + core) % ROW == 0)
+    short = has_far & jnp.logical_not(long)
     fsurf = (fx, fy, fz)
+    esurf = (ex, ey, ez)
     hsurf = (hx, hy, hz)
-    me = space * 2 + core
-    after = me + 1
-    before = me - 1
-    has_after = after < total
-    has_before = before >= 0
-    after_id = (after // 2, after % 2)
-    before_id = (lax.max(before, 0) // 2, lax.max(before, 0) % 2)
+    sums = (px, py, pz)
+    far_sums = (qx, qy, qz)
 
     barrier = pltpu.get_barrier_semaphore()
-
-    @pl.when(has_after)
+    pl.semaphore_signal(barrier, inc=1, device_id=mate_id, device_id_type=MESH)
+
+    @pl.when(has_far)
     def _():
-        pl.semaphore_signal(barrier, inc=1, device_id=after_id, device_id_type=MESH)
-
-    @pl.when(has_before)
-    def _():
-        pl.semaphore_signal(barrier, inc=1, device_id=before_id, device_id_type=MESH)
+        pl.semaphore_signal(barrier, inc=1, device_id=far_id, device_id_type=MESH)
 
     local = [
         pltpu.make_async_copy(feat, own, lsem.at[0]),
@@ -160,10 +167,8 @@
     for copy in local:
         copy.start()
 
-    for surf in fsurf + hsurf:
+    for surf in fsurf + esurf + hsurf:
         surf[0] = jnp.zeros((64, 2 * C), BF16)
-    cols[0] = jnp.zeros((64, 9 * C), BF16)
-    cols[9] = jnp.zeros((64, 9 * C), BF16)
 
     local[0].wait()
     for x in range(8):
@@ -171,101 +176,144 @@
     for axis in range(3):
         pack_pair(fsurf[axis].at[2], acc, lambda v: v.astype(BF16), axis)
 
-    def unpack(stage, weights):
-        @pl.loop(0, 3)
-        def _(i):
-            for jk in range(9):
-                tile = stage[i, jk // 3, jk % 3]
-                weights[core, 9 * i + jk, 0:48, :] = tile[:, 0:C]
-                weights[core, 9 * i + jk, 48:96, :] = tile[:, C:2 * C]
-
-    local[3].wait()
-    unpack(stage1, w1)
-
-    pl.semaphore_wait(barrier, has_after.astype(jnp.int32) + has_before.astype(jnp.int32))
+    def unpack(stage, weights, i):
+        for jk in range(9):
+            tile = stage[i, jk // 3, jk % 3]
+            weights[core, 9 * i + jk, 0:48, :] = tile[:, 0:C]
+            weights[core, 9 * i + jk, 48:96, :] = tile[:, C:2 * C]
+
+    pl.semaphore_wait(barrier, 1 + has_far.astype(jnp.int32))
+
+    def remote(source, target, send, recv, device):
+        return pltpu.make_async_remote_copy(
+            src_ref=source, dst_ref=target, send_sem=send, recv_sem=recv,
+            device_id=device, device_id_type=MESH)
 
     def sends(surf, sems, recvs, axis):
-        ahead = pltpu.make_async_remote_copy(
-            src_ref=surf[axis].at[2], dst_ref=surf[axis].at[1],
-            send_sem=sems.at[0, axis], recv_sem=recvs.at[0, axis],
-            device_id=after_id, device_id_type=MESH)
-        back = pltpu.make_async_remote_copy(
-            src_ref=surf[axis].at[2], dst_ref=surf[axis].at[3],
-            send_sem=sems.at[1, axis], recv_sem=recvs.at[1, axis],
-            device_id=before_id, device_id_type=MESH)
-        return ahead, back
+        return (
+            remote(surf[axis].at[2], surf[axis].at[1], sems.at[0, axis], recvs.at[0, axis], mate_id),
+            remote(surf[axis].at[2], surf[axis].at[3], sems.at[1, axis], recvs.at[1, axis], far_id),
+        )
 
     fcopies = [sends(fsurf, fsend, frecv, axis) for axis in range(3)]
     hcopies = [sends(hsurf, hsend, hrecv, axis) for axis in range(3)]
-
-    def start(pair):
-        pl.when(has_after)(pair[0].start)
-        pl.when(has_before)(pair[1].start)
-
-    def received(pair):
-        pl.when(has_before)(pair[0].wait_recv)
-        pl.when(has_after)(pair[1].wait_recv)
-
-    def sent(pair):
-        pl.when(has_after)(pair[0].wait_send)
-        pl.when(has_before)(pair[1].wait_send)
-
-    wcopies = [
-        pltpu.make_async_remote_copy(
-            src_ref=w.at[core], dst_ref=w.at[core], send_sem=wsend.at[n], recv_sem=wrecv.at[n],
-            device_id=(space, mate), device_id_type=MESH)
-        for n, w in enumerate((w1, w2))
-    ]
-    for pair in fcopies:
-        start(pair)
-    wcopies[0].start()
+    ecopies = [
+        remote(fsurf[axis].at[2], esurf[axis].at[1], fsend.at[1, axis], frecv.at[1, axis], far_id)
+        for axis in range(3)]
+    pcopies = [
+        remote(sums[axis], far_sums[axis], psend.at[axis], precv.at[axis], far_id) for axis in range(3)]
+    tcopy = remote(nbr, ftab, psend.at[3], precv.at[3], far_id)
+
+    def to_mate(part, n):
+        return remote(part, part, wsend.at[n], wrecv.at[n], mate_id)
+
+    order = (1, 0, 2)
+    wcopies = [to_mate(w1.at[core, pl.ds(9 * i, 9)], n) for n, i in enumerate(order)]
+    wcopies.append(to_mate(w2.at[core], 3))
+    for axis in range(3):
+        pl.when(short)(fcopies[axis][1].start)
+        pl.when(long)(ecopies[axis].start)
+        fcopies[axis][0].start()
+    pl.when(long)(tcopy.start)
+    local[3].wait()
+    for n, i in enumerate(order):
+        unpack(stage1, w1, i)
+        wcopies[n].start()
 
     local[1].wait()
     local[2].wait()
     where = []
     for t in range(27):
         n = tab[0, t]
-        where.append(jnp.where(n >= 0, jnp.clip(n - me + 2, 1, 3), 0))
+        where.append(jnp.where(n < 0, 0, jnp.where(n == me, 2, jnp.where(n == mate_slot, 1, 3))))
     active = occs[0].astype(F32)
 
-    own_columns(cols, own)
+    for x in range(8):
+        own_columns(cols.at[x], own[x])
     local[4].wait()
-    unpack(stage2, w2)
-    wcopies[1].start()
-    wcopies[0].wait_recv()
-    for half in range(2):
-        put(acc, slice(256 * half, 256 * half + 256), own_conv(cols, w1, half))
-    for axis in range(3):
-        received(fcopies[axis])
-        add_pair(acc, fcols, fsurf[axis], where, w1, axis)
+    for n, i in enumerate(order):
+        wcopies[n].wait_recv()
+        unpack(stage2, w2, i)
+        for first, last in (((1, 4), (4, 8)), ((0, 4), (4, 8)), ((0, 4), (4, 7)))[i]:
+            rows = slice(64 * first, 64 * last)
+            d = own_product(cols, w1, i, first, last)
+            put(acc, rows, get(acc, rows) + d if n else d)
+    wcopies[3].start()
+
+    @pl.when(jnp.logical_not(long))
+    def _():
+        def arrived(axis):
+            fcopies[axis][0].wait_recv()
+            pl.when(short)(fcopies[axis][1].wait_recv)
+
+        add_faces(acc, fcols, fsurf, where, w1, arrived)
+
+    @pl.when(long)
+    def _():
+        near = [jnp.where(w == 3, 0, w) for w in where]
+        add_faces(acc, fcols, fsurf, near, w1, lambda axis: fcopies[axis][0].wait_recv())
+        for axis in range(3):
+            pack_pair(sums[axis], acc, lambda v: v, axis)
+            pcopies[axis].start()
+        away = [jnp.where(w == 3, 1, 0) for w in where]
+        add_faces(acc, fcols, esurf, away, w1, lambda axis: ecopies[axis].wait_recv())
 
     def hidden(v):
         return (jnp.maximum(v, 0.0) * active).astype(BF16)
 
     for axis in range(3):
         pack_pair(hsurf[axis].at[2], acc, hidden, axis)
-        start(hcopies[axis])
-
-    @pl.loop(0, 8)
-    def _(x):
-        v = hidden(get(acc, pl.ds(pl.multiple_of(64 * x, 64), 64)))
-        columns(cols.at[x + 1], 0.0, framed(v.astype(F32)), 0.0)
-
-    wcopies[1].wait_recv()
-    for half in range(2):
-        res = own[4 * half:4 * half + 4].reshape(256, C).astype(F32)
-        put(acc2, slice(256 * half, 256 * half + 256), res + own_conv(cols, w2, half))
+        pl.when(short)(hcopies[axis][1].start)
+        hcopies[axis][0].start()
+
+    wcopies[3].wait_recv()
+    for x in range(8):
+        own_columns(cols.at[x], hidden(get(acc, slice(64 * x, 64 * x + 64))))
+    res = own[0:4].reshape(256, C).astype(F32)
+    d = own_product(cols, w2, 1, 0, 4) + own_product(cols, w2, 2, 0, 4) + res
+    put(acc2, slice(0, 64), d[:64])
+    put(acc2, slice(64, 256), d[64:] + own_product(cols, w2, 0, 1, 4))
+    res = own[4:8].reshape(256, C).astype(F32)
+    d = own_product(cols, w2, 1, 4, 8) + own_product(cols, w2, 0, 4, 8) + res
+    put(acc2, slice(256, 448), d[:192] + own_product(cols, w2, 2, 4, 7))
+    put(acc2, slice(448, 512), d[192:])
     act[...] = jnp.full((8, C), active, F32)
+
+    @pl.when(long)
+    def _():
+        tcopy.wait_recv()
+        fetch = pltpu.make_async_copy(ftab, tab2, lsem.at[5])
+        fetch.start()
+        facc[...] = jnp.zeros((2, 512, 128), F32)
+        fetch.wait()
+        given = [jnp.where(tab2[0, t] == me, 2, 0) for t in range(27)]
+        add_faces(facc, fcols, fsurf, given, w1, lambda axis: None)
+        for axis in range(3):
+            pcopies[axis].wait_send()
+        for axis in range(3):
+            pack_pair(sums[axis], facc, lambda v: v, axis)
 
     for copy in wcopies:
         copy.wait_send()
-    for pair in fcopies:
-        sent(pair)
     for axis in range(3):
-        received(hcopies[axis])
-        add_pair(acc2, fcols, hsurf[axis], where, w2, axis)
-    for pair in hcopies:
-        sent(pair)
+        fcopies[axis][0].wait_send()
+        pl.when(short)(fcopies[axis][1].wait_send)
+        pl.when(long)(ecopies[axis].wait_send)
+    pl.when(long)(tcopy.wait_send)
+
+    def arrived(axis):
+        hcopies[axis][0].wait_recv()
+        pl.when(short)(hcopies[axis][1].wait_recv)
+
+        @pl.when(long)
+        def _():
+            pcopies[axis].wait_recv()
+            hsurf[axis][3] = jnp.maximum(far_sums[axis][...] + sums[axis][...], 0.0).astype(BF16)
+
+    add_faces(acc2, fcols, hsurf, where, w2, arrived)
+    for near, away in hcopies:
+        near.wait_send()
+        pl.when(short)(away.wait_send)
 
 
 def finish_kernel(acc2, act, out, done, sem):
@@ -299,23 +347,31 @@
         out_specs=(vmem,) * 2,
         scratch_shapes=[
             pltpu.VMEM((8, 64, C), BF16),
-            *[pltpu.VMEM((4, 64, 2 * C), BF16)] * 6,
+            *[pltpu.VMEM((4, 64, 2 * C), BF16)] * 3,
+            *[pltpu.VMEM((2, 64, 2 * C), BF16)] * 3,
+            *[pltpu.VMEM((4, 64, 2 * C), BF16)] * 3,
             pltpu.VMEM((3, 3, 3, 48, 2 * C), BF16),
             pltpu.VMEM((3, 3, 3, 48, 2 * C), BF16),
             pltpu.VMEM((2, 27, 96, C), BF16),
             pltpu.VMEM((2, 27, 96, C), BF16),
-            pltpu.VMEM((10, 64, 9 * C), BF16),
+            pltpu.VMEM((8, 64, 9 * C), BF16),
             pltpu.VMEM((6, 64, 9 * C), BF16),
             pltpu.VMEM((2, 512, 128), F32),
+            pltpu.VMEM((2, 512, 128), F32),
+            *[pltpu.VMEM((64, 2 * C), F32)] * 6,
+            pltpu.VMEM((1, 27), jnp.int32),
+            pltpu.SMEM((1, 27), jnp.int32),
             pltpu.SMEM((1, 27), jnp.int32),
             pltpu.SMEM((1,), jnp.int32),
-            pltpu.SemaphoreType.DMA((5,)),
+            pltpu.SemaphoreType.DMA((6,)),
             pltpu.SemaphoreType.DMA((2, 3)),
             pltpu.SemaphoreType.DMA((2, 3)),
-            pltpu.SemaphoreType.DMA((2,)),
-            pltpu.SemaphoreType.DMA((2,)),
+            pltpu.SemaphoreType.DMA((4,)),
+            pltpu.SemaphoreType.DMA((4,)),
             pltpu.SemaphoreType.DMA((2, 3)),
             pltpu.SemaphoreType.DMA((2, 3)),
+            pltpu.SemaphoreType.DMA((4,)),
+            pltpu.SemaphoreType.DMA((4,)),
         ],
         compiler_params=pltpu.CompilerParams(
             collective_id=0, has_side_effects=True, vmem_limit_bytes=32 * 1024 * 1024),

time: 21.8 us -> 19.9 us (0.913)
  the two profiles are of different devices: /device:TPU:1 before, /device:TPU:320 now
where the time goes in v4:
time: 19.9 us; the launch traced here: 19.8 us
  Pallas kernels  19.1 us (96%)
  between operations  0.66 us (3%)
    pallas_call x1, Pallas kernels, body(): pl.pallas_call(functools.partial(exchange_kernel, total), out_shape=(pltp...  18.3 us
    pallas_call x1, Pallas kernels, body(): pl.pallas_call(finish_kernel, out_shape=jax.ShapeDtypeStruct((8, 64, C),...  0.83 us

profile of v4, /device:TPU:320, one launch (start us, length us, event | category | flops | bytes accessed | tf_op | source)
XLA Modules:
  0.0 19.8 jit_solution(12466022954100218409)
XLA Ops:
  0.7 18.3 %shard_map.55 = (f32[2,512,128]{2,1,0:T(8,128)S(1)}, f32[8,192]{1,0:T(8,128)S(1)}) custom-call(bf16[8,64,192]{2,1,0:T(8,128)(2,1)} %bitcast.2, s32[1]{0:T(128)S(6)} %copy.6.occ, s32[1,27]{1,0:T(1,128)} %nbr.1, bf16[3,3,3,48,384]{4,3,2,1,0:T(8,128)(2,1)} %wk1.1, bf16[3,3,3,48,384]{4,3,2,1,0:T(8,128)(2,1)} %wk2.1), custom_call_target="tpu_custom_call" | custom-call | tf_op jit(solution)/shard_map/pallas_call | solution.py:340
  18.9 0.8 %shard_map.56 = f32[8,64,192]{2,1,0:T(8,128)} custom-call(f32[2,512,128]{2,1,0:T(8,128)S(1)} %get-tuple-element.7.acc2, f32[8,192]{1,0:T(8,128)S(1)} %get-tuple-element.8.act), custom_call_target="tpu_custom_call" | custom-call | tf_op jit(solution)/shard_map/pallas_call | solution.py:379

commit v5 on v4

--- a/solution.py
+++ b/solution.py
@@ -127,8 +127,8 @@
 def exchange_kernel(
     total, feat, occ, nbr, wk1, wk2,
     acc2, act,
-    own, fx, fy, fz, ex, ey, ez, hx, hy, hz, stage1, stage2, w1, w2, cols, fcols, acc, facc,
-    px, py, pz, qx, qy, qz, ftab, tab, tab2, occs,
+    own, fx, fy, fz, ex, ey, ez, hx, hy, hz, stage1, mate1, stage2, w1, w2, cols, fcols, acc, facc,
+    px, py, pz, qx, qy, qz, gx, gy, gz, ftab, tab, tab2, occs,
     lsem, fsend, frecv, wsend, wrecv, hsend, hrecv, psend, precv,
 ):
     space = lax.axis_index("space")
@@ -144,11 +144,15 @@
     mate_id = (space, mate)
     long = has_far & ((space + core) % ROW == 0)
     short = has_far & jnp.logical_not(long)
+    early = long | (has_far & ((space + core) % 4 == 0)) | (me == 1)
+    first = long & (core == 0)
+    second = long & (core == 1)
     fsurf = (fx, fy, fz)
     esurf = (ex, ey, ez)
     hsurf = (hx, hy, hz)
     sums = (px, py, pz)
     far_sums = (qx, qy, qz)
+    given_sums = (gx, gy, gz)
 
     barrier = pltpu.get_barrier_semaphore()
     pl.semaphore_signal(barrier, inc=1, device_id=mate_id, device_id_type=MESH)
@@ -170,19 +174,11 @@
     for surf in fsurf + esurf + hsurf:
         surf[0] = jnp.zeros((64, 2 * C), BF16)
 
-    local[0].wait()
-    for x in range(8):
-        put(acc, slice(64 * x, 64 * x + 64), own[x].astype(F32))
-    for axis in range(3):
-        pack_pair(fsurf[axis].at[2], acc, lambda v: v.astype(BF16), axis)
-
-    def unpack(stage, weights, i):
+    def unpack(stage, weights, h, i):
         for jk in range(9):
             tile = stage[i, jk // 3, jk % 3]
-            weights[core, 9 * i + jk, 0:48, :] = tile[:, 0:C]
-            weights[core, 9 * i + jk, 48:96, :] = tile[:, C:2 * C]
-
-    pl.semaphore_wait(barrier, 1 + has_far.astype(jnp.int32))
+            weights[h, 9 * i + jk, 0:48, :] = tile[:, 0:C]
+            weights[h, 9 * i + jk, 48:96, :] = tile[:, C:2 * C]
 
     def remote(source, target, send, recv, device):
         return pltpu.make_async_remote_copy(
@@ -204,21 +200,77 @@
         remote(sums[axis], far_sums[axis], psend.at[axis], precv.at[axis], far_id) for axis in range(3)]
     tcopy = remote(nbr, ftab, psend.at[3], precv.at[3], far_id)
 
-    def to_mate(part, n):
-        return remote(part, part, wsend.at[n], wrecv.at[n], mate_id)
-
     order = (1, 0, 2)
-    wcopies = [to_mate(w1.at[core, pl.ds(9 * i, 9)], n) for n, i in enumerate(order)]
-    wcopies.append(to_mate(w2.at[core], 3))
+    wcopies = [
+        remote(wk1.at[i], mate1.at[i], wsend.at[n], wrecv.at[n], mate_id) for n, i in enumerate(order)]
+    for n, i in enumerate(order):
+        part = w2.at[core, pl.ds(9 * i, 9)]
+        wcopies.append(remote(part, part, wsend.at[3 + n], wrecv.at[3 + n], mate_id))
+
+    def prepare_faces():
+        local[0].wait()
+        for x in range(8):
+            put(acc, slice(64 * x, 64 * x + 64), own[x].astype(F32))
+        for axis in range(3):
+            pack_pair(fsurf[axis].at[2], acc, lambda v: v.astype(BF16), axis)
+
+    def prepare_own():
+        for x in range(8):
+            own_columns(cols.at[x], own[x])
+        local[3].wait()
+        for i in order:
+            unpack(stage1, w1, core, i)
+
+    def unpack_two():
+        local[4].wait()
+        for i in order:
+            unpack(stage2, w2, core, i)
+
+    def send_two():
+        for n in range(3):
+            wcopies[3 + n].start()
+
+    def own_part(with_two=True, send=True):
+        if with_two:
+            local[4].wait()
+        for n, i in enumerate(order):
+            wcopies[n].wait_recv()
+            unpack(mate1, w1, mate, i)
+            if with_two:
+                unpack(stage2, w2, core, i)
+            for start, stop in (((1, 4), (4, 8)), ((0, 4), (4, 8)), ((0, 4), (4, 7)))[i]:
+                rows = slice(64 * start, 64 * stop)
+                d = own_product(cols, w1, i, start, stop)
+                put(acc, rows, get(acc, rows) + d if n else d)
+            if send:
+                wcopies[3 + n].start()
+
+    @pl.when(early)
+    def _():
+        prepare_faces()
+        prepare_own()
+
+    pl.when(first)(functools.partial(own_part, True, False))
+    pl.semaphore_wait(barrier, 1 + has_far.astype(jnp.int32))
+
+    @pl.when(jnp.logical_not(early))
+    def _():
+        for n in range(3):
+            wcopies[n].start()
+        prepare_faces()
+
+    pl.when(long)(tcopy.start)
     for axis in range(3):
         pl.when(short)(fcopies[axis][1].start)
         pl.when(long)(ecopies[axis].start)
         fcopies[axis][0].start()
-    pl.when(long)(tcopy.start)
-    local[3].wait()
-    for n, i in enumerate(order):
-        unpack(stage1, w1, i)
-        wcopies[n].start()
+
+    @pl.when(early)
+    def _():
+        for n in range(3):
+            wcopies[n].start()
+
+    pl.when(jnp.logical_not(early))(prepare_own)
 
     local[1].wait()
     local[2].wait()
@@ -228,17 +280,9 @@
         where.append(jnp.where(n < 0, 0, jnp.where(n == me, 2, jnp.where(n == mate_slot, 1, 3))))
     active = occs[0].astype(F32)
 
-    for x in range(8):
-        own_columns(cols.at[x], own[x])
-    local[4].wait()
-    for n, i in enumerate(order):
-        wcopies[n].wait_recv()
-        unpack(stage2, w2, i)
-        for first, last in (((1, 4), (4, 8)), ((0, 4), (4, 8)), ((0, 4), (4, 7)))[i]:
-            rows = slice(64 * first, 64 * last)
-            d = own_product(cols, w1, i, first, last)
-            put(acc, rows, get(acc, rows) + d if n else d)
-    wcopies[3].start()
+    pl.when(jnp.logical_not(long))(own_part)
+    pl.when(second)(functools.partial(own_part, False, False))
+    pl.when(first)(send_two)
 
     @pl.when(jnp.logical_not(long))
     def _():
@@ -253,8 +297,23 @@
         near = [jnp.where(w == 3, 0, w) for w in where]
         add_faces(acc, fcols, fsurf, near, w1, lambda axis: fcopies[axis][0].wait_recv())
         for axis in range(3):
-            pack_pair(sums[axis], acc, lambda v: v, axis)
+            pack_pair(sums[axis], acc, lambda v: v.astype(BF16), axis)
             pcopies[axis].start()
+
+        @pl.when(second)
+        def _():
+            unpack_two()
+            send_two()
+
+        tcopy.wait_recv()
+        fetch = pltpu.make_async_copy(ftab, tab2, lsem.at[5])
+        fetch.start()
+        facc[...] = jnp.zeros((2, 512, 128), F32)
+        fetch.wait()
+        given = [jnp.where(tab2[0, t] == me, 2, 0) for t in range(27)]
+        add_faces(facc, fcols, fsurf, given, w1, lambda axis: None)
+        for axis in range(3):
+            pack_pair(given_sums[axis], facc, lambda v: v, axis)
         away = [jnp.where(w == 3, 1, 0) for w in where]
         add_faces(acc, fcols, esurf, away, w1, lambda axis: ecopies[axis].wait_recv())
 
@@ -266,7 +325,8 @@
         pl.when(short)(hcopies[axis][1].start)
         hcopies[axis][0].start()
 
-    wcopies[3].wait_recv()
+    for n in range(3):
+        wcopies[3 + n].wait_recv()
     for x in range(8):
         own_columns(cols.at[x], hidden(get(acc, slice(64 * x, 64 * x + 64))))
     res = own[0:4].reshape(256, C).astype(F32)
@@ -279,27 +339,18 @@
     put(acc2, slice(448, 512), d[192:])
     act[...] = jnp.full((8, C), active, F32)
 
-    @pl.when(long)
-    def _():
-        tcopy.wait_recv()
-        fetch = pltpu.make_async_copy(ftab, tab2, lsem.at[5])
-        fetch.start()
-        facc[...] = jnp.zeros((2, 512, 128), F32)
-        fetch.wait()
-        given = [jnp.where(tab2[0, t] == me, 2, 0) for t in range(27)]
-        add_faces(facc, fcols, fsurf, given, w1, lambda axis: None)
-        for axis in range(3):
-            pcopies[axis].wait_send()
-        for axis in range(3):
-            pack_pair(sums[axis], facc, lambda v: v, axis)
-
     for copy in wcopies:
         copy.wait_send()
     for axis in range(3):
         fcopies[axis][0].wait_send()
         pl.when(short)(fcopies[axis][1].wait_send)
         pl.when(long)(ecopies[axis].wait_send)
-    pl.when(long)(tcopy.wait_send)
+
+    @pl.when(long)
+    def _():
+        tcopy.wait_send()
+        for axis in range(3):
+            pcopies[axis].wait_send()
 
     def arrived(axis):
         hcopies[axis][0].wait_recv()
@@ -308,7 +359,8 @@
         @pl.when(long)
         def _():
             pcopies[axis].wait_recv()
-            hsurf[axis][3] = jnp.maximum(far_sums[axis][...] + sums[axis][...], 0.0).astype(BF16)
+            hsurf[axis][3] = jnp.maximum(
+                far_sums[axis][...].astype(F32) + given_sums[axis][...], 0.0).astype(BF16)
 
     add_faces(acc2, fcols, hsurf, where, w2, arrived)
     for near, away in hcopies:
@@ -350,15 +402,15 @@
             *[pltpu.VMEM((4, 64, 2 * C), BF16)] * 3,
             *[pltpu.VMEM((2, 64, 2 * C), BF16)] * 3,
             *[pltpu.VMEM((4, 64, 2 * C), BF16)] * 3,
-            pltpu.VMEM((3, 3, 3, 48, 2 * C), BF16),
-            pltpu.VMEM((3, 3, 3, 48, 2 * C), BF16),
+            *[pltpu.VMEM((3, 3, 3, 48, 2 * C), BF16)] * 3,
             pltpu.VMEM((2, 27, 96, C), BF16),
             pltpu.VMEM((2, 27, 96, C), BF16),
             pltpu.VMEM((8, 64, 9 * C), BF16),
             pltpu.VMEM((6, 64, 9 * C), BF16),
             pltpu.VMEM((2, 512, 128), F32),
             pltpu.VMEM((2, 512, 128), F32),
-            *[pltpu.VMEM((64, 2 * C), F32)] * 6,
+            *[pltpu.VMEM((64, 2 * C), BF16)] * 6,
+            *[pltpu.VMEM((64, 2 * C), F32)] * 3,
             pltpu.VMEM((1, 27), jnp.int32),
             pltpu.SMEM((1, 27), jnp.int32),
             pltpu.SMEM((1, 27), jnp.int32),
@@ -366,8 +418,8 @@
             pltpu.SemaphoreType.DMA((6,)),
             pltpu.SemaphoreType.DMA((2, 3)),
             pltpu.SemaphoreType.DMA((2, 3)),
-            pltpu.SemaphoreType.DMA((4,)),
-            pltpu.SemaphoreType.DMA((4,)),
+            pltpu.SemaphoreType.DMA((6,)),
+            pltpu.SemaphoreType.DMA((6,)),
             pltpu.SemaphoreType.DMA((2, 3)),
             pltpu.SemaphoreType.DMA((2, 3)),
             pltpu.SemaphoreType.DMA((4,)),

time: 19.9 us -> 19.3 us (0.970)
  the two profiles are of different devices: /device:TPU:320 before, /device:TPU:255 now
where the time goes in v5:
time: 19.3 us; the launch traced here: 19.1 us
  Pallas kernels  18.3 us (95%)
  between operations  0.82 us (4%)
    pallas_call x1, Pallas kernels, body(): pl.pallas_call(functools.partial(exchange_kernel, total), out_shape=(pltp...  17.5 us
    pallas_call x1, Pallas kernels, body(): pl.pallas_call(finish_kernel, out_shape=jax.ShapeDtypeStruct((8, 64, C),...  0.83 us

profile of v5, /device:TPU:255, one launch (start us, length us, event | category | flops | bytes accessed | tf_op | source)
XLA Modules:
  0.0 19.1 jit_solution(5830699077575222535)
XLA Ops:
  0.7 17.5 %shard_map.55 = (f32[2,512,128]{2,1,0:T(8,128)S(1)}, f32[8,192]{1,0:T(8,128)S(1)}) custom-call(bf16[8,64,192]{2,1,0:T(8,128)(2,1)} %bitcast.2, s32[1]{0:T(128)S(6)} %copy.6.occ, s32[1,27]{1,0:T(1,128)} %nbr.1, bf16[3,3,3,48,384]{4,3,2,1,0:T(8,128)(2,1)} %wk1.1, bf16[3,3,3,48,384]{4,3,2,1,0:T(8,128)(2,1)} %wk2.1), custom_call_target="tpu_custom_call" | custom-call | tf_op jit(solution)/shard_map/pallas_call | solution.py:392
  18.1 0.8 %shard_map.56 = f32[8,64,192]{2,1,0:T(8,128)} custom-call(f32[2,512,128]{2,1,0:T(8,128)S(1)} %get-tuple-element.7.acc2, f32[8,192]{1,0:T(8,128)S(1)} %get-tuple-element.8.act), custom_call_target="tpu_custom_call" | custom-call | tf_op jit(solution)/shard_map/pallas_call | solution.py:431

commit v6 on v5

--- a/solution.py
+++ b/solution.py
@@ -11,7 +11,7 @@
 MESH = pl.DeviceIdType.MESH
 F32 = jnp.float32
 BF16 = jnp.bfloat16
-ROW = 32
+ROW = 16
 FACES = ((-1, 0, 0), (1, 0, 0), (0, -1, 0), (0, 1, 0), (0, 0, -1), (0, 0, 1))
 
 
@@ -145,7 +145,7 @@
     long = has_far & ((space + core) % ROW == 0)
     short = has_far & jnp.logical_not(long)
     early = long | (has_far & ((space + core) % 4 == 0)) | (me == 1)
-    first = long & (core == 0)
+    first = long & (core == 0) & (space % 32 == 0) & (space % 128 != 0)
     second = long & (core == 1)
     fsurf = (fx, fy, fz)
     esurf = (ex, ey, ez)
@@ -280,7 +280,7 @@
         where.append(jnp.where(n < 0, 0, jnp.where(n == me, 2, jnp.where(n == mate_slot, 1, 3))))
     active = occs[0].astype(F32)
 
-    pl.when(jnp.logical_not(long))(own_part)
+    pl.when(jnp.logical_not(first | second))(own_part)
     pl.when(second)(functools.partial(own_part, False, False))
     pl.when(first)(send_two)
 

time: 19.3 us -> 18.9 us (0.979)
  the two profiles are of different devices: /device:TPU:255 before, /device:TPU:1 now
where the time goes in v6:
time: 18.9 us; the launch traced here: 18.8 us
  Pallas kernels  18 us (95%)
  between operations  0.82 us (4%)
    pallas_call x1, Pallas kernels, body(): pl.pallas_call(functools.partial(exchange_kernel, total), out_shape=(pltp...  17.1 us
    pallas_call x1, Pallas kernels, body(): pl.pallas_call(finish_kernel, out_shape=jax.ShapeDtypeStruct((8, 64, C),...  0.83 us

profile of v6, /device:TPU:1, one launch (start us, length us, event | category | flops | bytes accessed | tf_op | source)
XLA Modules:
  0.0 18.8 jit_solution(11177887693582508998)
XLA Ops:
  0.7 17.1 %shard_map.55 = (f32[2,512,128]{2,1,0:T(8,128)S(1)}, f32[8,192]{1,0:T(8,128)S(1)}) custom-call(bf16[8,64,192]{2,1,0:T(8,128)(2,1)} %bitcast.2, s32[1]{0:T(128)S(6)} %copy.6.occ, s32[1,27]{1,0:T(1,128)} %nbr.1, bf16[3,3,3,48,384]{4,3,2,1,0:T(8,128)(2,1)} %wk1.1, bf16[3,3,3,48,384]{4,3,2,1,0:T(8,128)(2,1)} %wk2.1), custom_call_target="tpu_custom_call" | custom-call | tf_op jit(solution)/shard_map/pallas_call | solution.py:392
  17.8 0.8 %shard_map.56 = f32[8,64,192]{2,1,0:T(8,128)} custom-call(f32[2,512,128]{2,1,0:T(8,128)S(1)} %get-tuple-element.7.acc2, f32[8,192]{1,0:T(8,128)S(1)} %get-tuple-element.8.act), custom_call_target="tpu_custom_call" | custom-call | tf_op jit(solution)/shard_map/pallas_call | solution.py:431

commit v7 on v6

--- a/solution.py
+++ b/solution.py
@@ -127,7 +127,7 @@
 def exchange_kernel(
     total, feat, occ, nbr, wk1, wk2,
     acc2, act,
-    own, fx, fy, fz, ex, ey, ez, hx, hy, hz, stage1, mate1, stage2, w1, w2, cols, fcols, acc, facc,
+    own, fx, fy, fz, ex, ey, ez, hx, hy, hz, stage1, mate1, stage2, mate2, w1, w2, cols, fcols, acc, facc,
     px, py, pz, qx, qy, qz, gx, gy, gz, ftab, tab, tab2, occs,
     lsem, fsend, frecv, wsend, wrecv, hsend, hrecv, psend, precv,
 ):
@@ -147,6 +147,8 @@
     early = long | (has_far & ((space + core) % 4 == 0)) | (me == 1)
     first = long & (core == 0) & (space % 32 == 0) & (space % 128 != 0)
     second = long & (core == 1)
+    raw = me == 0
+    ready = me == 1
     fsurf = (fx, fy, fz)
     esurf = (ex, ey, ez)
     hsurf = (hx, hy, hz)
@@ -206,6 +208,14 @@
     for n, i in enumerate(order):
         part = w2.at[core, pl.ds(9 * i, 9)]
         wcopies.append(remote(part, part, wsend.at[3 + n], wrecv.at[3 + n], mate_id))
+
+    rcopies = [
+        remote(wk2.at[i], mate2.at[i], wsend.at[3 + n], wrecv.at[3 + n], mate_id)
+        for n, i in enumerate(order)]
+
+    def start_raw():
+        for copy in rcopies:
+            copy.start()
 
     def prepare_faces():
         local[0].wait()
@@ -250,6 +260,7 @@
         prepare_faces()
         prepare_own()
 
+    pl.when(ready)(unpack_two)
     pl.when(first)(functools.partial(own_part, True, False))
     pl.semaphore_wait(barrier, 1 + has_far.astype(jnp.int32))
 
@@ -257,6 +268,7 @@
     def _():
         for n in range(3):
             wcopies[n].start()
+        pl.when(raw)(start_raw)
         prepare_faces()
 
     pl.when(long)(tcopy.start)
@@ -270,6 +282,7 @@
         for n in range(3):
             wcopies[n].start()
 
+    pl.when(ready)(send_two)
     pl.when(jnp.logical_not(early))(prepare_own)
 
     local[1].wait()
@@ -280,8 +293,8 @@
         where.append(jnp.where(n < 0, 0, jnp.where(n == me, 2, jnp.where(n == mate_slot, 1, 3))))
     active = occs[0].astype(F32)
 
-    pl.when(jnp.logical_not(first | second))(own_part)
-    pl.when(second)(functools.partial(own_part, False, False))
+    pl.when(jnp.logical_not(first | second | ready | raw))(own_part)
+    pl.when(second | ready | raw)(functools.partial(own_part, False, False))
     pl.when(first)(send_two)
 
     @pl.when(jnp.logical_not(long))
@@ -325,8 +338,19 @@
         pl.when(short)(hcopies[axis][1].start)
         hcopies[axis][0].start()
 
-    for n in range(3):
-        wcopies[3 + n].wait_recv()
+    pl.when(raw)(unpack_two)
+
+    @pl.when(ready)
+    def _():
+        for n, i in enumerate(order):
+            rcopies[n].wait_recv()
+            unpack(mate2, w2, mate, i)
+
+    @pl.when(jnp.logical_not(ready))
+    def _():
+        for n in range(3):
+            wcopies[3 + n].wait_recv()
+
     for x in range(8):
         own_columns(cols.at[x], hidden(get(acc, slice(64 * x, 64 * x + 64))))
     res = own[0:4].reshape(256, C).astype(F32)
@@ -339,8 +363,10 @@
     put(acc2, slice(448, 512), d[192:])
     act[...] = jnp.full((8, C), active, F32)
 
-    for copy in wcopies:
-        copy.wait_send()
+    for n in range(3):
+        wcopies[n].wait_send()
+        pl.when(raw)(rcopies[n].wait_send)
+        pl.when(jnp.logical_not(raw))(wcopies[3 + n].wait_send)
     for axis in range(3):
         fcopies[axis][0].wait_send()
         pl.when(short)(fcopies[axis][1].wait_send)
@@ -402,7 +428,7 @@
             *[pltpu.VMEM((4, 64, 2 * C), BF16)] * 3,
             *[pltpu.VMEM((2, 64, 2 * C), BF16)] * 3,
             *[pltpu.VMEM((4, 64, 2 * C), BF16)] * 3,
-            *[pltpu.VMEM((3, 3, 3, 48, 2 * C), BF16)] * 3,
+            *[pltpu.VMEM((3, 3, 3, 48, 2 * C), BF16)] * 4,
             pltpu.VMEM((2, 27, 96, C), BF16),
             pltpu.VMEM((2, 27, 96, C), BF16),
             pltpu.VMEM((8, 64, 9 * C), BF16),

time: 18.9 us -> 19 us (level)
  no operation moved by 1% of the time
where the time goes in v7:
time: 19 us; the launch traced here: 18.9 us
  Pallas kernels  18.1 us (95%)
  between operations  0.82 us (4%)
    pallas_call x1, Pallas kernels, body(): pl.pallas_call(functools.partial(exchange_kernel, total), out_shape=(pltp...  17.2 us
    pallas_call x1, Pallas kernels, body(): pl.pallas_call(finish_kernel, out_shape=jax.ShapeDtypeStruct((8, 64, C),...  0.83 us

profile of v7, /device:TPU:1, one launch (start us, length us, event | category | flops | bytes accessed | tf_op | source)
XLA Modules:
  0.0 18.9 jit_solution(9094642721740193186)
XLA Ops:
  0.7 17.2 %shard_map.55 = (f32[2,512,128]{2,1,0:T(8,128)S(1)}, f32[8,192]{1,0:T(8,128)S(1)}) custom-call(bf16[8,64,192]{2,1,0:T(8,128)(2,1)} %bitcast.2, s32[1]{0:T(128)S(6)} %copy.6.occ, s32[1,27]{1,0:T(1,128)} %nbr.1, bf16[3,3,3,48,384]{4,3,2,1,0:T(8,128)(2,1)} %wk1.1, bf16[3,3,3,48,384]{4,3,2,1,0:T(8,128)(2,1)} %wk2.1), custom_call_target="tpu_custom_call" | custom-call | tf_op jit(solution)/shard_map/pallas_call | solution.py:418
  17.9 0.8 %shard_map.56 = f32[8,64,192]{2,1,0:T(8,128)} custom-call(f32[2,512,128]{2,1,0:T(8,128)S(1)} %get-tuple-element.7.acc2, f32[8,192]{1,0:T(8,128)S(1)} %get-tuple-element.8.act), custom_call_target="tpu_custom_call" | custom-call | tf_op jit(solution)/shard_map/pallas_call | solution.py:457

commit v8 on v6

--- a/solution.py
+++ b/solution.py
@@ -259,13 +259,18 @@
             wcopies[n].start()
         prepare_faces()
 
+    @pl.when(me == 1)
+    def _():
+        for n in range(3):
+            wcopies[n].start()
+
     pl.when(long)(tcopy.start)
     for axis in range(3):
         pl.when(short)(fcopies[axis][1].start)
         pl.when(long)(ecopies[axis].start)
         fcopies[axis][0].start()
 
-    @pl.when(early)
+    @pl.when(early & (me != 1))
     def _():
         for n in range(3):
             wcopies[n].start()

time: 18.9 us -> 18.9 us (level)
  no operation moved by 1% of the time
where the time goes in v8:
time: 18.9 us; the launch traced here: 18.8 us
  Pallas kernels  18 us (95%)
  between operations  0.82 us (4%)
    pallas_call x1, Pallas kernels, body(): pl.pallas_call(functools.partial(exchange_kernel, total), out_shape=(pltp...  17.1 us
    pallas_call x1, Pallas kernels, body(): pl.pallas_call(finish_kernel, out_shape=jax.ShapeDtypeStruct((8, 64, C),...  0.83 us

profile of v8, /device:TPU:1, one launch (start us, length us, event | category | flops | bytes accessed | tf_op | source)
XLA Modules:
  0.0 18.8 jit_solution(18421931219282067910)
XLA Ops:
  0.7 17.1 %shard_map.55 = (f32[2,512,128]{2,1,0:T(8,128)S(1)}, f32[8,192]{1,0:T(8,128)S(1)}) custom-call(bf16[8,64,192]{2,1,0:T(8,128)(2,1)} %bitcast.2, s32[1]{0:T(128)S(6)} %copy.6.occ, s32[1,27]{1,0:T(1,128)} %nbr.1, bf16[3,3,3,48,384]{4,3,2,1,0:T(8,128)(2,1)} %wk1.1, bf16[3,3,3,48,384]{4,3,2,1,0:T(8,128)(2,1)} %wk2.1), custom_call_target="tpu_custom_call" | custom-call | tf_op jit(solution)/shard_map/pallas_call | solution.py:397
  17.8 0.8 %shard_map.56 = f32[8,64,192]{2,1,0:T(8,128)} custom-call(f32[2,512,128]{2,1,0:T(8,128)S(1)} %get-tuple-element.7.acc2, f32[8,192]{1,0:T(8,128)S(1)} %get-tuple-element.8.act), custom_call_target="tpu_custom_call" | custom-call | tf_op jit(solution)/shard_map/pallas_call | solution.py:436
